TPU v7x, 256 devices: a whole 4x4x8 slice. The times are simulated.
256 devices in a mesh: row: 128 (over z, y, x), col: 2 (over core).
Axes of the slice: x: 4, y: 4, z: 8, core: 2. Of those that a mesh axis runs over, the one named last changes fastest.
Arguments:
- panel_column: float32 [2, 32768, 256], P(None, 'row'), may hold values from -9 to 201, as said below
- trailing: float32 [2, 32768, 1, 512], P(None, 'row', None, 'col'), may hold values from -6 to 262
Outputs:
- panel_factor: float32 [2, 32768, 256], P(None, 'row')
- updated: float32 [2, 32768, 1, 512], P(None, 'row', None, 'col')
- next_panel: float32 [2, 32768, 256], P(None, 'row', 'col')
Inputs may be any that keep to these rules, and one draw needn't show every extreme that they name: The first 256 rows of panel_column form a symmetric positive definite block; the rows 256 to 512 of the first 256 columns of updated form a block whose symmetric part is positive definite.
All inputs are finite; a program needn't handle non-finite values.
Results may differ from a plain program's by a relative error of at most 0.00005.
Values sent between devices are 32-bit elements; how exact they have to be, the bound alone decides.
No kernel may reach another device: no remote copies, remote signals or barrier semaphores. Data moves between devices by JAX's collectives and lax.ppermute only.
A program may use at most 64 MiB of HBM per device.

v0:
```python
import jax
import jax.numpy as jnp
from jax import lax
from jax.sharding import PartitionSpec as P


def spread(value, axis, source):
    kept = jnp.where(lax.axis_index(axis) == source, value, 0).astype(value.dtype)
    return lax.psum(kept, axis)


def lower_factor(square):
    return jnp.linalg.cholesky(0.5 * (square + square.T))


def solve_blocks(factor, blocks):
    flat = blocks.reshape(-1, blocks.shape[-1])
    result = jax.scipy.linalg.solve_triangular(factor, flat.T, lower=True).T
    return result.reshape(blocks.shape)


def on_device(panel_column, trailing):
    row_count = lax.axis_size("row")
    col_count = lax.axis_size("col")
    row_index = lax.axis_index("row")
    col_index = lax.axis_index("col")
    slot_count = panel_column.shape[0]
    panel_width = panel_column.shape[1]
    col_slots = trailing.shape[2]
    count_all = col_slots * col_count
    block_ids = jnp.arange(slot_count, dtype=jnp.int32) * row_count + row_index
    is_first = (block_ids == 0)[:, None, None]
    diag_top = spread(panel_column[0], "row", 0)
    factor = lower_factor(diag_top)
    solved = solve_blocks(factor, panel_column)
    carried_early = jnp.where(is_first, 0.0, solved)

    def fetch_block(position, buffer):
        target = position + 1
        piece_in = lax.dynamic_index_in_dim(carried_early, target // row_count, 0, keepdims=False)
        piece_in = spread(piece_in, "row", target % row_count)
        return lax.dynamic_update_index_in_dim(buffer, piece_in, position, 0)

    buffer = lax.fori_loop(
        0, count_all, fetch_block, jnp.zeros((count_all, panel_width, panel_width), jnp.float32)
    )
    grouped = buffer.reshape(col_slots, col_count, panel_width, panel_width)
    columns = lax.dynamic_index_in_dim(grouped, col_index, 1, keepdims=False)
    panel_factor = jnp.where(is_first, factor[None], solved)
    carried = jnp.where(is_first, 0.0, solved)
    rows_flat = carried.reshape(slot_count * panel_width, panel_width)
    cols_flat = columns.reshape(col_slots * panel_width, panel_width)
    change = jnp.dot(
        rows_flat, cols_flat.T, precision=lax.Precision.HIGHEST, preferred_element_type=jnp.float32
    )
    updated = trailing - change.reshape(trailing.shape)
    lead_column = updated[:, :, 0, :]
    corner = lead_column[1 // row_count]
    corner = spread(corner, "row", 1 % row_count)
    corner = jnp.where(col_index == 0, corner, jnp.eye(panel_width, dtype=jnp.float32))
    factor_next = lower_factor(corner)
    solved_next = solve_blocks(factor_next, lead_column)
    next_local = jnp.where((block_ids == 1)[:, None, None], factor_next[None], solved_next)
    next_local = jnp.where(is_first, 0.0, next_local)
    forwarded = spread(next_local, "col", 0)
    half_width = panel_width // col_count
    next_panel = lax.dynamic_slice_in_dim(forwarded, col_index * half_width, half_width, 2)
    return (panel_factor, updated, next_panel)


def solution(mesh):
    return jax.shard_map(
        on_device,
        mesh=mesh,
        in_specs=(P(None, "row", None), P(None, "row", None, "col")),
        out_specs=(P(None, "row", None), P(None, "row", None, "col"), P(None, "row", "col")),
        check_vma=False,
    )
```

profile of v0, /device:TPU:1, one launch (start us, length us, event | category | flops | bytes accessed | tf_op | source)
XLA Modules:
  0.0 1060.8 jit_solution(12865998741229493848)
XLA Ops:
  7.2 0.0 all-reduce.6.cloned.1.call-start
  7.2 1.7 select_bitcast_fusion
  8.9 0.0 all-reduce.6.cloned.1.call-update
  8.9 0.1 broadcast_in_dim.91
  9.0 220.0 %all-reduce.6.cloned.1.call-done = f32[256,256]{1,0:T(8,128)} async-done(((f32[256,256]{1,0:T(8,128)}), f32[256,256]{1,0:T(8,128)}) %all-reduce.6.cloned.1.call-update) | async-done | bytes 262160 | tf_op jit(solution)/shard_map/psum | solution.py:9
  229.0 1.1 copy.5
  230.2 0.1 copy.6
  230.4 11.7 %cholesky.130 = f32[128,128]{1,0:T(8,128)S(1)} custom-call(f32[128,128]{1,0:T(8,128)S(1)} %cholesky.194), custom_call_target="Cholesky" | custom-call | tf_op jit(solution)/shard_map/jit(cholesky)/cholesky | solution.py:13
  242.2 9.8 custom-call.13
  252.0 0.2 constant_dynamic-update-slice_fusion.2
  252.2 0.3 convolution_subtract_fusion.3
  252.5 11.7 %cholesky.147 = f32[128,128]{1,0:T(8,128)S(1)} custom-call(f32[128,128]{1,0:T(8,128)S(1)} %convolution_subtract_fusion.3), custom_call_target="Cholesky" | custom-call | tf_op jit(solution)/shard_map/jit(cholesky)/cholesky | solution.py:13
  264.2 0.6 compare_reduce_fusion.2
  266.2 0.1 triangular_solve.75
  266.3 4.2 while.23
  266.5 0.6 fusion.40
  267.1 1.4 bitcast_dynamic-update-slice_fusion.6
  268.5 0.6 fusion.40
  269.1 1.4 bitcast_dynamic-update-slice_fusion.6
  270.5 19.7 %custom-call.14 = f32[2,128,128]{1,2,0:T(8,128)S(1)} custom-call(f32[2,128,128]{2,1,0:T(8,128)S(1)} %get-tuple-element.112), custom_call_target="InvertDiagBlocksLowerTriangular" | custom-call | tf_op jit(solution)/shard_map/jit(_solve_triangular)/triangular_solve | solution.py:18
  290.2 0.4 fusion.4
  290.6 0.6 convolution_subtract_fusion.1
  291.2 0.4 fusion.19
  291.7 0.2 copy.17
  292.0 0.2 copy.15
  292.2 0.9 broadcast_select_fusion
  293.1 442.1 %while.22 = (s32[]{:T(128)}, f32[2,256,256]{2,1,0:T(8,128)S(1)}, f32[2,256,256]{2,1,0:T(8,128)S(1)}) while((s32[]{:T(128)}, f32[2,256,256]{2,1,0:T(8,128)S(1)}, f32[2,256,256]{2,1,0:T(8,128)S(1)}) %tuple.96), condition=%wide.region_7.10_spmd.clone, body=%wide.region_5.9_spmd.sunk.clone | while | flops 131100 | bytes 2621804 | solution.py:44
  293.1 0.7 dynamic-slice_select_fusion.3
  293.8 0.0 all-reduce.12.cloned.1.call-update
  293.9 219.4 %all-reduce.12.cloned.1.call-done = f32[1,256,256]{2,1,0:T(8,128)} async-done(((f32[1,256,256]{2,1,0:T(8,128)}), f32[1,256,256]{2,1,0:T(8,128)}) %all-reduce.12.cloned.1.call-update) | async-done | bytes 262160 | tf_op jit(solution)/shard_map/while/body/eval_jaxpr/psum | solution.py:9
  513.2 1.0 constant_dynamic-update-slice_fusion.7
  514.2 0.0 all-reduce.12.cloned.1.call-start
  514.3 0.7 dynamic-slice_select_fusion.3
  515.0 219.2 %all-reduce.12.cloned.1.call-done = f32[1,256,256]{2,1,0:T(8,128)} async-done(((f32[1,256,256]{2,1,0:T(8,128)}), f32[1,256,256]{2,1,0:T(8,128)}) %all-reduce.12.cloned.1.call-update) | async-done | bytes 262160 | tf_op jit(solution)/shard_map/while/body/eval_jaxpr/psum | solution.py:9
  734.2 1.0 constant_dynamic-update-slice_fusion.7
  735.2 0.0 all-reduce.8.cloned.1.call-start
  735.3 0.6 fusion
  735.9 0.7 fusion.3
  736.7 0.0 all-reduce.10.cloned.1.call-start
  736.7 218.2 %all-reduce.8.cloned.1.call-done = f32[256,256]{1,0:T(8,128)} async-done(((f32[256,256]{1,0:T(8,128)}), f32[256,256]{1,0:T(8,128)}) %all-reduce.8.cloned.1.call-update) | async-done | bytes 262160 | tf_op jit(solution)/shard_map/psum | solution.py:9
  955.0 0.1 copy.11
  955.1 0.8 copy-done.2
  956.0 0.1 copy.12
  956.2 11.7 %cholesky.164 = f32[128,128]{1,0:T(8,128)S(1)} custom-call(f32[128,128]{1,0:T(8,128)S(1)} %cholesky.197), custom_call_target="Cholesky" | custom-call | tf_op jit(solution)/shard_map/jit(cholesky)/cholesky | solution.py:13
  968.0 9.8 custom-call.15
  977.8 0.2 constant_dynamic-update-slice_fusion.1
  978.0 0.3 convolution_subtract_fusion.2
  978.3 11.7 %cholesky.181 = f32[128,128]{1,0:T(8,128)S(1)} custom-call(f32[128,128]{1,0:T(8,128)S(1)} %convolution_subtract_fusion.2), custom_call_target="Cholesky" | custom-call | tf_op jit(solution)/shard_map/jit(cholesky)/cholesky | solution.py:13
  990.0 0.6 compare_reduce_fusion.1
  990.7 0.7 compare_reduce_fusion
  992.8 4.3 while.24
  993.0 0.6 fusion.41
  993.6 1.4 bitcast_dynamic-update-slice_fusion.7
  995.1 0.6 fusion.41
  995.7 1.4 bitcast_dynamic-update-slice_fusion.7
  997.1 19.7 %custom-call.16 = f32[2,128,128]{1,2,0:T(8,128)S(1)} custom-call(f32[2,128,128]{2,1,0:T(8,128)S(1)} %get-tuple-element.113), custom_call_target="InvertDiagBlocksLowerTriangular" | custom-call | tf_op jit(solution)/shard_map/jit(_solve_triangular)/triangular_solve | solution.py:18
  1016.8 0.4 fusion.1
  1017.2 0.6 convolution_subtract_fusion
  1017.8 0.4 fusion.15
  1018.3 0.2 copy.16
  1018.5 0.9 select_select_fusion
  1019.5 1.3 copy.14
  1020.8 31.8 %all-reduce.10.cloned.1.call-done = f32[2,256,256]{2,1,0:T(8,128)} async-done(((f32[2,256,256]{2,1,0:T(8,128)}), f32[2,256,256]{2,1,0:T(8,128)}) %all-reduce.10.cloned.1.call-update) | async-done | bytes 524304 | tf_op jit(solution)/shard_map/psum | solution.py:9
  1052.6 1.7 constant_dynamic-slice_fusion.2
  (40 shorter events, 0.7 us)
Async XLA Ops:
  7.2 221.9 %all-reduce.6.cloned.1.call-start = ((), (), s32[]{:S(2)}) async-start(), calls=%async_computation | async-start | bytes 524288 | tf_op jit(solution)/shard_map/psum | solution.py:9
  229.0 1.2 copy-start.1
  266.2 24.0 %copy-start = (f32[2,256,256]{2,1,0:T(8,128)S(1)}, f32[2,256,256]{2,1,0:T(8,128)}, u32[]{:S(2)}) copy-start(f32[2,256,256]{2,1,0:T(8,128)} %param.7) | copy-start | bytes 1572868
  293.1 442.2 %copy-start.3 = (f32[2,256,1,256]{3,2,1,0:T(1,128)S(1)}, f32[2,256,1,256]{3,2,1,0:T(1,128)}, u32[]{:S(2)}) copy-start(f32[2,256,1,256]{3,2,1,0:T(1,128)} %param.8) | copy-start | bytes 1572868
  293.1 220.1 %all-reduce.12.cloned.1.call-start = ((), (), s32[]{:S(2)}) async-start(), calls=%async_computation.3 | async-start | bytes 524288 | tf_op jit(solution)/shard_map/while/body/eval_jaxpr/psum | solution.py:9
  514.2 220.0 %all-reduce.12.cloned.1.call-start = ((), (), s32[]{:S(2)}) async-start(), calls=%async_computation.3 | async-start | bytes 524288 | tf_op jit(solution)/shard_map/while/body/eval_jaxpr/psum | solution.py:9
  735.2 219.8 %all-reduce.8.cloned.1.call-start = ((), (), s32[]{:S(2)}) async-start(), calls=%async_computation.1 | async-start | bytes 524288 | tf_op jit(solution)/shard_map/psum | solution.py:9
  736.7 316.0 %all-reduce.10.cloned.1.call-start = ((), (), s32[]{:S(2)}) async-start(), calls=%async_computation.2 | async-start | bytes 1048576 | tf_op jit(solution)/shard_map/psum | solution.py:9
  955.0 1.0 copy-start.2
Sparse Core Ops, SparseCore 0:
  13.9 215.0 all-reduce.5
  299.9 213.2 all-reduce.11
  521.0 213.2 all-reduce.11
  741.7 213.2 all-reduce.7
  1019.6 33.0 all-reduce.9
where the time goes:
time: 1060 us
  waiting for transfers between devices  909 us (86%)
  other arithmetic  114 us (11%)
  between operations  16.8 us (2%)
  local copies, waits for them, and re-layouts  16.1 us (2%)
    psum x5, waiting for transfers between devices, spread(): return lax.psum(kept, axis)  909 us
    another operation x13, other arithmetic, lower_factor(): return jnp.linalg.cholesky(0.5 * (square + square.T))  68.6 us
    another operation x4, other arithmetic, solve_blocks(): result = jax.scipy.linalg.solve_triangular(factor, flat.T, lower=True).T  39.4 us
  transfers between devices with their start and end apart: 5, of which 5 were waited for; matrix products, arithmetic and copies ran while one was open for 0% of the time, Pallas kernels for 0%

commit v1 on v0

v1 whole, which is shorter than its diff:
```python
import functools

import jax
import jax.numpy as jnp
from jax import lax
from jax.experimental import pallas as pl
from jax.experimental.pallas import tpu as pltpu
from jax.sharding import Mesh, PartitionSpec as P

N = 256
NB = 16
STEPS = N // NB


def dot_nt(a, b):
    return lax.dot_general(
        a, b, (((1,), (1,)), ((), ())),
        precision=lax.Precision.HIGHEST, preferred_element_type=jnp.float32,
    )


def dot_nn(a, b):
    return lax.dot_general(
        a, b, (((1,), (0,)), ((), ())),
        precision=lax.Precision.HIGHEST, preferred_element_type=jnp.float32,
    )


def factor_inverse(w, spl, xb, zb, tt):
    lane = lax.broadcasted_iota(jnp.int32, (NB, N), 1)
    sub = lax.broadcasted_iota(jnp.int32, (NB, N), 0)
    lane_all = lax.broadcasted_iota(jnp.int32, (N, N), 1)
    row_all = lax.broadcasted_iota(jnp.int32, (N, N), 0)
    zb[...] = jnp.zeros((NB, N), jnp.float32)
    tt[...] = jnp.zeros((N, NB), jnp.float32)

    def step(b, carry):
        r0 = pl.multiple_of(b * NB, NB)
        rows = w[pl.ds(r0, NB), :]
        half = jnp.where(b < STEPS // 2, rows[:, :128], rows[:, 128:])
        base = lax.rem(r0, 128)
        for j in range(NB):
            idx = jnp.full((NB, 128), base + j, jnp.int32)
            spl[j] = jnp.take_along_axis(half, idx, axis=1)
        in_block = (lane >= r0) & (lane < r0 + NB)
        unit = jnp.where(lane - r0 == sub, 1.0, 0.0)
        xb[...] = jnp.where(in_block, unit, rows)
        z_old = zb[...]
        late = dot_nn(tt[...], z_old)
        old = w[...]
        gone = (lane_all >= r0 - NB) & (lane_all < r0)
        w[...] = jnp.where(row_all >= r0 + NB, jnp.where(gone, 0.0, old) - late, old)
        s = [[spl[j, i:i + 1, :] for j in range(i + 1)] for i in range(NB)]
        x = [[xb[i:i + 1, 128 * h:128 * h + 128] for h in range(2)] for i in range(NB)]
        for k in range(NB):
            r = lax.rsqrt(s[k][k])
            y = [x[k][h] * r for h in range(2)]
            for h in range(2):
                zb[k:k + 1, 128 * h:128 * h + 128] = y[h]
            col = [None] * NB
            for i in range(k + 1, NB):
                col[i] = s[i][k] * r
                for j in range(k + 1, i + 1):
                    s[i][j] = s[i][j] - col[i] * col[j]
                for h in range(2):
                    x[i][h] = x[i][h] - col[i] * y[h]
        z = zb[...]
        tt[...] = jnp.where(lane >= r0 + NB, z, 0.0).T
        n0 = pl.multiple_of(jnp.minimum(r0 + NB, N - NB), NB)
        near = w[pl.ds(n0, NB), :]
        near = jnp.where(in_block, 0.0, near) - dot_nn(tt[pl.ds(n0, NB), :], z)
        w[pl.ds(n0, NB), :] = near
        w[pl.ds(r0, NB), :] = z
        return carry

    lax.fori_loop(0, STEPS, step, 0)
    return jnp.where(lane_all <= row_all, w[...], 0.0)


def kernel(flags, mine, other, panel, trail, trail_other, pf, up, nx, w, spl, xb, zb, tt):
    row, core = flags[0], flags[1]
    is0 = core == 0
    lane_all = lax.broadcasted_iota(jnp.int32, (N, N), 1)
    row_all = lax.broadcasted_iota(jnp.int32, (N, N), 0)
    low = lane_all <= row_all

    def both(lo, hi):
        m, o = mine[:, lo:hi, :], other[:, lo:hi, :]
        size = 16 * (hi - lo)
        return jnp.where(is0, m, o).reshape(size, N), jnp.where(is0, o, m).reshape(size, N)

    head = jnp.concatenate(both(0, 8), 0)
    corner, block1 = both(8, 24)
    block2 = jnp.concatenate(both(24, 32), 0)
    head = 0.5 * (head + head.T)
    w[...] = head
    inv1 = factor_inverse(w, spl, xb, zb, tt)
    below1 = dot_nt(block1, inv1)
    below_own = dot_nt(jnp.where(is0, block1, block2), inv1)
    corner = corner - dot_nt(below1, below1)
    corner = 0.5 * (corner + corner.T)
    w[...] = corner
    for slot in range(2):
        rows = pl.ds(slot * N, N)
        first = (row == 0) if slot == 0 else False
        solved = dot_nt(panel[rows, :], inv1)
        carried = solved
        if slot == 0:
            solved = jnp.where(first & ~low, 0.0, solved)
            carried = jnp.where(first, 0.0, solved)
        pf[rows, :] = solved
        up[rows, :] = trail[rows, :] - dot_nt(carried, below_own)
        lead = jnp.where(is0, trail[rows, :], trail_other[rows, :]) - dot_nt(carried, below1)
        if slot == 0:
            lead = jnp.where(row == 1, corner, lead)
        trail_other[rows, :] = lead
    inv2 = factor_inverse(w, spl, xb, zb, tt)
    half = jnp.where(is0, inv2[:128], inv2[128:])
    low_half = lane_all[:, :128] + core * 128 <= row_all[:, :128]
    for slot in range(2):
        rows = pl.ds(slot * N, N)
        solved = dot_nt(trail_other[rows, :], half)
        if slot == 0:
            solved = jnp.where((row == 0) | ((row == 1) & ~low_half), 0.0, solved)
        nx[rows, :] = solved


def local_part(flags, mine, other, panel, trail, trail_other):
    vmem = pl.BlockSpec(memory_space=pltpu.VMEM)
    f32 = jnp.float32
    return pl.pallas_call(
        kernel,
        out_shape=[
            jax.ShapeDtypeStruct((512, N), f32),
            jax.ShapeDtypeStruct((512, N), f32),
            jax.ShapeDtypeStruct((512, 128), f32),
        ],
        in_specs=[pl.BlockSpec(memory_space=pltpu.SMEM)] + [vmem] * 5,
        out_specs=[vmem] * 3,
        scratch_shapes=[
            pltpu.VMEM((N, N), f32),
            pltpu.VMEM((NB, NB, 128), f32),
            pltpu.VMEM((NB, N), f32),
            pltpu.VMEM((NB, N), f32),
            pltpu.VMEM((N, NB), f32),
        ],
        compiler_params=pltpu.CompilerParams(vmem_limit_bytes=40 << 20),
        name="panel_step",
    )(flags, mine, other, panel, trail, trail_other)


def on_device(panel, trail):
    plane = ("y", "x")
    z = lax.axis_index("z")
    member = lax.axis_index(plane)
    core = lax.axis_index("core")
    row = z * lax.axis_size(plane) + member
    trail_other = lax.ppermute(trail.reshape(512, N), "core", [(0, 1), (1, 0)])
    block = panel[0]
    part = lax.dynamic_slice_in_dim(block, core * 128, 128, 0).reshape(16, 8, N)
    part = jnp.concatenate([part, jnp.zeros_like(part)], 1)
    full = jnp.where(core == 0, trail[0, :, 0, :], block).reshape(16, 16, N)
    sent = jnp.where(row == 1, full, part)
    got = lax.all_to_all(sent, plane, 0, 0)
    piece = jnp.concatenate([got[0, :8], got[1], got[2, :8]], 0)
    piece = jnp.where(z == 0, piece, 0.0)
    size = lax.axis_size("z")
    reach = 1
    while reach < size:
        piece = piece + lax.ppermute(piece, "z", [(i, i + reach) for i in range(reach)])
        reach *= 2
    mine = lax.all_to_all(jnp.broadcast_to(piece[None], (16, 32, N)), plane, 0, 0)
    other = lax.ppermute(mine, "core", [(0, 1), (1, 0)])
    flags = jnp.stack([row, core]).astype(jnp.int32)
    pf, up, nx = local_part(
        flags, mine, other, panel.reshape(512, N), trail.reshape(512, N), trail_other
    )
    return pf.reshape(2, N, N), up.reshape(2, N, 1, N), nx.reshape(2, N, 128)


def solution(mesh):
    grid = Mesh(mesh.devices.reshape(8, 4, 4, 2), ("z", "y", "x", "core"))
    rows = ("z", "y", "x")
    return jax.shard_map(
        on_device,
        mesh=grid,
        in_specs=(P(None, rows, None), P(None, rows, None, "core")),
        out_specs=(P(None, rows, None), P(None, rows, None, "core"), P(None, rows, "core")),
        check_vma=False,
    )
```

time: 1060 us -> 80 us (0.08)
  waiting for transfers between devices: 909 us -> 17.9 us
  other arithmetic: 114 us -> 0.85 us
  Pallas kernels: 0 us -> 28.9 us
  starting transfers between devices: 0.17 us -> 26.6 us
  between operations: 16.8 us -> 0.76 us
  local copies, waits for them, and re-layouts: 16.1 us -> 4.18 us
    psum x5 -> x0, waiting for transfers between devices: 909 us -> none  [spread(): return lax.psum(kept, axis)]
    another operation x17 -> x1, other arithmetic: 108 us -> 0.07 us  [on_device(): flags = jnp.stack([row, core]).astype(jnp.int32)]
    pallas_call x0 -> x1, Pallas kernels: none -> 28.9 us  [local_part(): pl.pallas_call(kernel, out_shape=[jax.ShapeDtypeStruct((512, N), f32), ja...]
    ppermute x0 -> x5, starting transfers between devices: none -> 15.3 us  [the longest x3 8.17 us: on_device(): lax.ppermute(piece, 'z', [(i, i + reach) for i in range(reach)])]
    all_to_all x0 -> x2, waiting for transfers between devices: none -> 13.4 us  [the longest x1 7.54 us: on_device(): got = lax.all_to_all(sent, plane, 0, 0)]
    all_to_all x0 -> x2, starting transfers between devices: none -> 11.3 us  [the longest x1 7.57 us: on_device(): got = lax.all_to_all(sent, plane, 0, 0)]
  transfers between devices with their start and end apart: 5 -> 7, of which waited for: 5 -> 6; matrix products, arithmetic and copies ran while one was open for 0% -> 0% of each run, Pallas kernels for 0% -> 0%
where the time goes in v1:
time: 80 us; the launch traced here: 79.1 us
  Pallas kernels  28.9 us (36%)
  starting transfers between devices  26.6 us (33%)
  waiting for transfers between devices  17.9 us (22%)
  local copies, waits for them, and re-layouts  4.18 us (5%)
  other arithmetic  0.85 us (1%)
    pallas_call x1, Pallas kernels, local_part(): pl.pallas_call(kernel, out_shape=[jax.ShapeDtypeStruct((512, N), f32), ja...  28.9 us
    ppermute x3, starting transfers between devices, on_device(): lax.ppermute(piece, 'z', [(i, i + reach) for i in range(reach)])  8.17 us
    all_to_all x1, starting transfers between devices, on_device(): got = lax.all_to_all(sent, plane, 0, 0)  7.57 us
    all_to_all x1, waiting for transfers between devices, on_device(): got = lax.all_to_all(sent, plane, 0, 0)  7.54 us
    all_to_all x1, waiting for transfers between devices, on_device(): lax.all_to_all(jnp.broadcast_to(piece[None], (16, 32, N)), plane, 0, 0)  5.84 us
    ppermute x1, starting transfers between devices, on_device(): other = lax.ppermute(mine, 'core', [(0, 1), (1, 0)])  4.11 us
    all_to_all x1, starting transfers between devices, on_device(): lax.all_to_all(jnp.broadcast_to(piece[None], (16, 32, N)), plane, 0, 0)  3.71 us
    ppermute x1, starting transfers between devices, on_device(): trail_other = lax.ppermute(trail.reshape(512, N), 'core', [(0, 1), (1, 0)])  3.05 us
  transfers between devices with their start and end apart: 7, of which 6 were waited for; matrix products, arithmetic and copies ran while one was open for 0% of the time, Pallas kernels for 0%

profile of v1, /device:TPU:1, one launch (start us, length us, event | category | flops | bytes accessed | tf_op | source)
XLA Modules:
  0.0 79.1 jit_solution(2103110529553279044)
XLA Ops:
  0.6 1.0 %slice.16 = f32[1,256,256]{2,1,0:T(8,128)S(1)} slice(f32[2,256,256]{2,1,0:T(8,128)} %param.2), slice={[0:1], [0:256], [0:256]} | slice | bytes 524288 | tf_op jit(solution)/shard_map/slice | solution.py:159
  1.6 0.0 slice-start
  1.6 0.9 %slice-done = f32[1,256,1,256]{3,2,1,0:T(1,128)S(1)} async-done(((f32[2,256,1,256]{3,2,1,0:T(1,128)}), f32[1,256,1,256]{3,2,1,0:T(1,128)S(1)}, s32[]{:S(2)}) %slice-start) | async-done | bytes 262168 | tf_op jit(solution)/shard_map/slice | solution.py:162
  2.6 0.8 pad_select_fusion
  3.4 7.6 %all-to-all-start = ((f32[16,16,256]{2,1,0:T(8,128)}), f32[16,16,256]{2,1,0:T(8,128)S(1)}, u32[]{:S(2)}, u32[]{:S(2)}) async-start(f32[16,16,256]{2,1,0:T(8,128)} %pad_select_fusion), calls=%async_computation | async-start | bytes 524288 | tf_op jit(solution)/shard_map/all_to_all | solution.py:164
  11.0 7.5 %all-to-all-done = f32[16,16,256]{2,1,0:T(8,128)S(1)} async-done(((f32[16,16,256]{2,1,0:T(8,128)}), f32[16,16,256]{2,1,0:T(8,128)S(1)}, u32[]{:S(2)}, u32[]{:S(2)}) %all-to-all-start) | async-done | bytes 262176 | tf_op jit(solution)/shard_map/all_to_all | solution.py:164
  18.5 3.5 %collective-permute-start = (f32[32,256]{1,0:T(8,128)S(1)}, f32[32,256]{1,0:T(8,128)S(1)}, u32[]{:S(2)}, u32[]{:S(2)}) collective-permute-start(f32[32,256]{1,0:T(8,128)S(1)} %maximum_select_fusion), channel_id=1, source_target_pairs={{0,32},{1,33},{2,34},{3,35},{4,36},{5,37},{6,38},{7,39},{8,40},{9,... | collective-permute-start | bytes 98312 | tf_op jit(solution)/shard_map/ppermute | solution.py:170
  22.1 1.0 %collective-permute-done = f32[32,256]{1,0:T(8,128)S(1)} collective-permute-done((f32[32,256]{1,0:T(8,128)S(1)}, f32[32,256]{1,0:T(8,128)S(1)}, u32[]{:S(2)}, u32[]{:S(2)}) %collective-permute-start) | collective-permute-done | bytes 32800 | tf_op jit(solution)/shard_map/ppermute | solution.py:170
  23.1 1.3 %collective-permute-start.1 = (f32[32,256]{1,0:T(8,128)S(1)}, f32[32,256]{1,0:T(8,128)S(1)}, u32[]{:S(2)}, u32[]{:S(2)}) collective-permute-start(f32[32,256]{1,0:T(8,128)S(1)} %add.23), channel_id=1, source_target_pairs={{0,64},{32,96},{1,65},{33,97},{2,66},{34,98},{3,67},{35,99},{4,68}... | collective-permute-start | bytes 98312 | tf_op jit(solution)/shard_map/ppermute | solution.py:170
  24.4 1.0 %collective-permute-done.1 = f32[32,256]{1,0:T(8,128)S(1)} collective-permute-done((f32[32,256]{1,0:T(8,128)S(1)}, f32[32,256]{1,0:T(8,128)S(1)}, u32[]{:S(2)}, u32[]{:S(2)}) %collective-permute-start.1) | collective-permute-done | bytes 32800 | tf_op jit(solution)/shard_map/ppermute | solution.py:170
  25.4 3.3 %collective-permute-start.2 = (f32[32,256]{1,0:T(8,128)S(1)}, f32[32,256]{1,0:T(8,128)S(1)}, u32[]{:S(2)}, u32[]{:S(2)}) collective-permute-start(f32[32,256]{1,0:T(8,128)S(1)} %add.24), channel_id=1, source_target_pairs={{0,128},{32,160},{64,192},{96,224},{1,129},{33,161},{65,193},{97,2... | collective-permute-start | bytes 98312 | tf_op jit(solution)/shard_map/ppermute | solution.py:170
  28.7 1.0 %collective-permute-done.2 = f32[32,256]{1,0:T(8,128)S(1)} collective-permute-done((f32[32,256]{1,0:T(8,128)S(1)}, f32[32,256]{1,0:T(8,128)S(1)}, u32[]{:S(2)}, u32[]{:S(2)}) %collective-permute-start.2) | collective-permute-done | bytes 32800 | tf_op jit(solution)/shard_map/ppermute | solution.py:170
  29.7 0.8 %broadcast_in_dim.12 = f32[16,32,256]{2,1,0:T(8,128)} broadcast(f32[32,256]{1,0:T(8,128)S(1)} %add.25), dimensions={1,2} | broadcast | bytes 557056 | tf_op jit(solution)/shard_map/broadcast_in_dim | solution.py:172
  30.6 0.0 copy-start.1
  30.6 3.7 %all-to-all-start.1 = ((f32[16,32,256]{2,1,0:T(8,128)}), f32[16,32,256]{2,1,0:T(8,128)S(1)}, u32[]{:S(2)}, u32[]{:S(2)}) async-start(f32[16,32,256]{2,1,0:T(8,128)} %broadcast_in_dim.12), calls=%async_computation.1 | async-start | bytes 1048576 | tf_op jit(solution)/shard_map/all_to_all | solution.py:172
  34.3 0.0 copy-done.1
  34.3 0.0 copy-start
  34.4 3.0 %collective-permute-start.4 = (f32[512,256]{1,0:T(8,128)S(1)}, f32[512,256]{1,0:T(8,128)S(1)}, u32[]{:S(2)}, u32[]{:S(2)}) collective-permute-start(f32[512,256]{1,0:T(8,128)S(1)} %bitcast.17), channel_id=1, source_target_pairs={{0,1},{1,0},{2,3},{3,2},{4,5},{5,4},{6,7},{7,6},{8,9},{9,8},{10,11... | collective-permute-start | bytes 1572872 | tf_op jit(solution)/shard_map/ppermute | solution.py:158
  37.4 5.8 %all-to-all-done.1.mine = f32[16,32,256]{2,1,0:T(8,128)S(1)} async-done(((f32[16,32,256]{2,1,0:T(8,128)}), f32[16,32,256]{2,1,0:T(8,128)S(1)}, u32[]{:S(2)}, u32[]{:S(2)}) %all-to-all-start.1) | async-done | bytes 524320 | tf_op jit(solution)/shard_map/all_to_all | solution.py:172
  43.3 4.1 %collective-permute-start.3 = (f32[16,32,256]{2,1,0:T(8,128)S(1)}, f32[16,32,256]{2,1,0:T(8,128)S(1)}, u32[]{:S(2)}, u32[]{:S(2)}) collective-permute-start(f32[16,32,256]{2,1,0:T(8,128)S(1)} %all-to-all-done.1.mine), channel_id=1, source_target_pairs={{0,1},{1,0},{2,3},{3,2},{4,5},{5,4},{6,7},{7,6},{8,9},{9,8},{10,11... | collective-permute-start | bytes 1572872 | tf_op jit(solution)/shard_map/ppermute | solution.py:173
  47.4 0.1 pad_add_fusion.flags
  47.4 0.0 collective-permute-done.4.trail_other
  47.5 1.5 %collective-permute-done.3.other = f32[16,32,256]{2,1,0:T(8,128)S(1)} collective-permute-done((f32[16,32,256]{2,1,0:T(8,128)S(1)}, f32[16,32,256]{2,1,0:T(8,128)S(1)}, u32[]{:S(2)}, u32[]{:S(2)}) %collective-permute-start.3) | collective-permute-done | bytes 524320 | tf_op jit(solution)/shard_map/ppermute | solution.py:173
  48.9 0.0 copy-done
  48.9 28.9 %panel_step.1 = (f32[512,256]{1,0:T(8,128)}, f32[512,256]{1,0:T(8,128)S(1)}, f32[512,128]{1,0:T(8,128)}) custom-call(s32[2]{0:T(128)S(1)} %pad_add_fusion.flags, f32[16,32,256]{2,1,0:T(8,128)S(1)} %all-to-all-done.1.mine, f32[16,32,256]{2,1,0:T(8,128)S(1)} %collective-permute-done.3.other, f32[512,256]{1,0:T(8,128)S(1)} %bitcast.19, ...), custom_call_target="tpu_custom_call" | custom-call | tf_op jit(solution)/shard_map/panel_step/pallas_call | solution.py:131
  77.8 1.3 %copy.5 = f32[2,256,1,256]{3,2,1,0:T(1,128)} copy(f32[2,256,1,256]{3,1,0,2:T(8,128)S(1)} %bitcast.20) | data formatting | bytes 1048576
  (9 shorter events, 0.1 us)
Async XLA Ops:
  1.6 1.0 %slice-start = ((f32[2,256,1,256]{3,2,1,0:T(1,128)}), f32[1,256,1,256]{3,2,1,0:T(1,128)S(1)}, s32[]{:S(2)}) async-start(f32[2,256,1,256]{3,2,1,0:T(1,128)} %param.3), calls=%async_computation.2 | async-start | bytes 524288 | tf_op jit(solution)/shard_map/slice | solution.py:162
  3.4 15.1 %all-to-all-start = ((f32[16,16,256]{2,1,0:T(8,128)}), f32[16,16,256]{2,1,0:T(8,128)S(1)}, u32[]{:S(2)}, u32[]{:S(2)}) async-start(f32[16,16,256]{2,1,0:T(8,128)} %pad_select_fusion), calls=%async_computation | async-start | bytes 524288 | tf_op jit(solution)/shard_map/all_to_all | solution.py:164
  18.5 4.6 %collective-permute-start = (f32[32,256]{1,0:T(8,128)S(1)}, f32[32,256]{1,0:T(8,128)S(1)}, u32[]{:S(2)}, u32[]{:S(2)}) collective-permute-start(f32[32,256]{1,0:T(8,128)S(1)} %maximum_select_fusion), channel_id=1, source_target_pairs={{0,32},{1,33},{2,34},{3,35},{4,36},{5,37},{6,38},{7,39},{8,40},{9,... | collective-permute-start | bytes 98312 | tf_op jit(solution)/shard_map/ppermute | solution.py:170
  23.1 2.3 %collective-permute-start.1 = (f32[32,256]{1,0:T(8,128)S(1)}, f32[32,256]{1,0:T(8,128)S(1)}, u32[]{:S(2)}, u32[]{:S(2)}) collective-permute-start(f32[32,256]{1,0:T(8,128)S(1)} %add.23), channel_id=1, source_target_pairs={{0,64},{32,96},{1,65},{33,97},{2,66},{34,98},{3,67},{35,99},{4,68}... | collective-permute-start | bytes 98312 | tf_op jit(solution)/shard_map/ppermute | solution.py:170
  25.4 4.4 %collective-permute-start.2 = (f32[32,256]{1,0:T(8,128)S(1)}, f32[32,256]{1,0:T(8,128)S(1)}, u32[]{:S(2)}, u32[]{:S(2)}) collective-permute-start(f32[32,256]{1,0:T(8,128)S(1)} %add.24), channel_id=1, source_target_pairs={{0,128},{32,160},{64,192},{96,224},{1,129},{33,161},{65,193},{97,2... | collective-permute-start | bytes 98312 | tf_op jit(solution)/shard_map/ppermute | solution.py:170
  30.6 3.7 %copy-start.1 = (f32[2,256,1,256]{3,2,1,0:T(1,128)S(1)}, f32[2,256,1,256]{3,2,1,0:T(1,128)}, u32[]{:S(2)}) copy-start(f32[2,256,1,256]{3,2,1,0:T(1,128)} %param.3) | copy-start | bytes 1572868
  30.6 12.7 %all-to-all-start.1 = ((f32[16,32,256]{2,1,0:T(8,128)}), f32[16,32,256]{2,1,0:T(8,128)S(1)}, u32[]{:S(2)}, u32[]{:S(2)}) async-start(f32[16,32,256]{2,1,0:T(8,128)} %broadcast_in_dim.12), calls=%async_computation.1 | async-start | bytes 1048576 | tf_op jit(solution)/shard_map/all_to_all | solution.py:172
  34.3 14.6 %copy-start = (f32[2,256,256]{2,1,0:T(8,128)S(1)}, f32[2,256,256]{2,1,0:T(8,128)}, u32[]{:S(2)}) copy-start(f32[2,256,256]{2,1,0:T(8,128)} %param.2) | copy-start | bytes 1572868
  34.4 13.1 %collective-permute-start.4 = (f32[512,256]{1,0:T(8,128)S(1)}, f32[512,256]{1,0:T(8,128)S(1)}, u32[]{:S(2)}, u32[]{:S(2)}) collective-permute-start(f32[512,256]{1,0:T(8,128)S(1)} %bitcast.17), channel_id=1, source_target_pairs={{0,1},{1,0},{2,3},{3,2},{4,5},{5,4},{6,7},{7,6},{8,9},{9,8},{10,11... | collective-permute-start | bytes 1572872 | tf_op jit(solution)/shard_map/ppermute | solution.py:158
  43.3 5.6 %collective-permute-start.3 = (f32[16,32,256]{2,1,0:T(8,128)S(1)}, f32[16,32,256]{2,1,0:T(8,128)S(1)}, u32[]{:S(2)}, u32[]{:S(2)}) collective-permute-start(f32[16,32,256]{2,1,0:T(8,128)S(1)} %all-to-all-done.1.mine), channel_id=1, source_target_pairs={{0,1},{1,0},{2,3},{3,2},{4,5},{5,4},{6,7},{7,6},{8,9},{9,8},{10,11... | collective-permute-start | bytes 1572872 | tf_op jit(solution)/shard_map/ppermute | solution.py:173

commit v2 on v1

v2 whole, which is shorter than its diff:
```python
import functools

import jax
import jax.numpy as jnp
from jax import lax
from jax.experimental import pallas as pl
from jax.experimental.pallas import tpu as pltpu
from jax.sharding import Mesh, PartitionSpec as P

N = 256
NB = 16
STEPS = N // NB
Z_STEPS = (
    [(0, 1)],
    [(0, 7), (1, 2)],
    [(0, 5), (1, 4), (2, 3), (7, 6)],
)


def dot_nt(a, b):
    return lax.dot_general(
        a, b, (((1,), (1,)), ((), ())),
        precision=lax.Precision.HIGHEST, preferred_element_type=jnp.float32,
    )


def split(a):
    high = a.astype(jnp.bfloat16)
    return high, (a - high.astype(jnp.float32)).astype(jnp.bfloat16)


def dot_nt3(a, b):
    a_hi, a_lo = split(a)
    b_hi, b_lo = b

    def part(u, v):
        return lax.dot_general(u, v, (((1,), (1,)), ((), ())), preferred_element_type=jnp.float32)

    return part(a_hi, b_hi) + (part(a_hi, b_lo) + part(a_lo, b_hi))


def dot_nn(a, b):
    return lax.dot_general(
        a, b, (((1,), (0,)), ((), ())),
        precision=lax.Precision.HIGHEST, preferred_element_type=jnp.float32,
    )


def spread_row(ref, i, h):
    return jnp.broadcast_to(ref[i:i + 1, 128 * h:128 * h + 128], (8, 128))


def factor_inverse(w, inv, near, spl, low, mid, xb, zb, tt):
    lane = lax.broadcasted_iota(jnp.int32, (NB, N), 1)
    sub = lax.broadcasted_iota(jnp.int32, (NB, N), 0)
    zb[...] = jnp.zeros((NB, N), jnp.float32)
    near[...] = w[0:NB, :]

    def step(b, carry, top):
        r0 = pl.multiple_of(b * NB, NB)
        n0 = pl.multiple_of(jnp.minimum(r0 + NB, N - NB), NB)
        lo = 128 * top
        base = r0 - lo
        rows = near[...]
        half = rows[:, lo:lo + 128]

        def column(tile, j):
            idx = jnp.full((8, 128), base + j, jnp.int32)
            return jnp.take_along_axis(tile, idx, axis=1)

        for j in range(8):
            spl[8 * j:8 * j + 8, :] = column(half[:8], j)
        v = [[column(half[8:], j)] for j in range(8)]
        d = [column(half[8:], 8 + j) for j in range(8)]
        in_block = (lane >= r0) & (lane < r0 + NB)
        xb[...] = jnp.where(in_block, jnp.where(lane - r0 == sub, 1.0, 0.0), rows)
        z_old = zb[...]
        tt[lo:, :] = jnp.where(lane[:, lo:] >= r0 + NB, z_old[:, lo:], 0.0).T
        gone = (lane >= r0 - NB) & (lane < r0)
        nxt = jnp.where(gone, 0.0, w[pl.ds(n0, NB), :]) - dot_nn(tt[pl.ds(n0, NB), :], z_old)
        for j in range(8):
            v[j] += [column(nxt[:8, lo:lo + 128], j), column(nxt[8:, lo:lo + 128], j)]
        c = [[column(nxt[8 * n:8 * n + 8, lo:lo + 128], 8 + j) for n in range(2)] for j in range(8)]
        nxt = jnp.where(in_block, 0.0, nxt)
        acc = [[nxt[8 * n:8 * n + 8, 128 * h:128 * h + 128] for h in range(2)] for n in range(2)]
        lane_r = lax.broadcasted_iota(jnp.int32, (N - lo, N), 1)
        row_r = lax.broadcasted_iota(jnp.int32, (N - lo, N), 0) + lo
        old = w[lo:, :]
        gone_r = (lane_r >= r0 - NB) & (lane_r < r0)
        w[lo:, :] = jnp.where(
            row_r >= r0 + NB, jnp.where(gone_r, 0.0, old) - dot_nn(tt[lo:, :], z_old), old
        )
        y_all = []
        for g in range(2):
            if g == 0:
                s = [[spread_row(spl, 8 * j + i, 0) for j in range(i + 1)] for i in range(8)]
            else:
                for j in range(8):
                    mid[8 * j:8 * j + 8, :] = d[j]
                s = [[spread_row(mid, 8 * j + i, 0) for j in range(i + 1)] for i in range(8)]
                v = c
            x = [[spread_row(xb, 8 * g + i, h) for h in range(2)] for i in range(8)]
            if g == 1:
                for k in range(8):
                    for i in range(8):
                        for h in range(2):
                            x[i][h] = x[i][h] - cross[k][i] * y_all[k][h]
            cross = []
            for k in range(8):
                r = lax.rsqrt(s[k][k])
                y = [x[k][h] * r for h in range(2)]
                y_all.append(y)
                for h in range(2):
                    zb[8 * g + k:8 * g + k + 1, 128 * h:128 * h + 128] = y[h][:1]
                col = [None] * 8
                for i in range(k + 1, 8):
                    col[i] = s[i][k] * r
                    for j in range(k + 1, i + 1):
                        s[i][j] = s[i][j] - col[i] * col[j]
                    for h in range(2):
                        x[i][h] = x[i][h] - col[i] * y[h]
                v[k] = [t * r for t in v[k]]
                for j in range(k + 1, 8):
                    v[j] = [t - u * col[j] for t, u in zip(v[j], v[k])]
                below = v[k]
                if g == 0:
                    low[8 * k:8 * k + 8, :] = v[k][0]
                    cross.append([spread_row(low, 8 * k + i, 0) for i in range(8)])
                    below = v[k][1:]
                    for j in range(8):
                        d[j] = d[j] - v[k][0] * cross[k][j]
                        c[j] = [t - u * cross[k][j] for t, u in zip(c[j], below)]
                for n in range(2):
                    for h in range(2):
                        acc[n][h] = acc[n][h] - below[n] * y[h]
        for n in range(2):
            for h in range(2):
                near[8 * n:8 * n + 8, 128 * h:128 * h + 128] = acc[n][h]
        inv[pl.ds(r0, NB), :] = jnp.where(lane - r0 <= sub, zb[...], 0.0)
        return carry

    for top in range(2):
        lax.fori_loop(top * STEPS // 2, (top + 1) * STEPS // 2, functools.partial(step, top=top), 0)


def kernel(flags, mine, other, panel, trail, trail_other, pf, up, nx, w, inv, *work):
    row, core = flags[0], flags[1]
    is0 = core == 0
    lane_all = lax.broadcasted_iota(jnp.int32, (N, N), 1)
    row_all = lax.broadcasted_iota(jnp.int32, (N, N), 0)
    low = lane_all <= row_all

    def pair(lo, hi):
        m, o = mine[:, lo:hi, :], other[:, lo:hi, :]
        return jnp.where(is0, m, o), jnp.where(is0, o, m)

    head = jnp.concatenate(pair(0, 8), 1).reshape(N, N)
    head = 0.5 * (head + head.T)
    w[...] = head
    factor_inverse(w, inv, *work)
    corner, block1 = [t.reshape(N, N) for t in pair(8, 24)]
    block2 = jnp.concatenate(pair(24, 32), 1).reshape(N, N)
    inv1 = inv[...]
    below1 = dot_nt(block1, inv1)
    corner = corner - dot_nt(below1, below1)
    corner = 0.5 * (corner + corner.T)
    w[...] = corner
    inv1 = split(inv1)
    below_own = split(jnp.where(is0, below1, dot_nt3(block2, inv1)))
    below1 = split(below1)
    for slot in range(2):
        rows = pl.ds(slot * N, N)
        solved = dot_nt3(panel[rows, :], inv1)
        carried = solved
        if slot == 0:
            first = row == 0
            solved = jnp.where(first & ~low, 0.0, solved)
            carried = jnp.where(first, 0.0, solved)
        pf[rows, :] = solved
        up[rows, :] = trail[rows, :] - dot_nt3(carried, below_own)
        lead = jnp.where(is0, trail[rows, :], trail_other[rows, :]) - dot_nt3(carried, below1)
        if slot == 0:
            lead = jnp.where(row == 1, corner, lead)
        trail_other[rows, :] = lead
    factor_inverse(w, inv, *work)
    half = split(inv[pl.ds(pl.multiple_of(core * 128, 128), 128), :])
    low_half = lane_all[:, :128] + core * 128 <= row_all[:, :128]
    for slot in range(2):
        rows = pl.ds(slot * N, N)
        solved = dot_nt3(trail_other[rows, :], half)
        if slot == 0:
            solved = jnp.where((row == 0) | ((row == 1) & ~low_half), 0.0, solved)
        nx[rows, :] = solved


def local_part(flags, mine, other, panel, trail, trail_other):
    vmem = pl.BlockSpec(memory_space=pltpu.VMEM)
    f32 = jnp.float32
    return pl.pallas_call(
        kernel,
        out_shape=[
            jax.ShapeDtypeStruct((512, N), f32),
            jax.ShapeDtypeStruct((512, N), f32),
            jax.ShapeDtypeStruct((512, 128), f32),
        ],
        in_specs=[pl.BlockSpec(memory_space=pltpu.SMEM)] + [vmem] * 5,
        out_specs=[vmem] * 3,
        scratch_shapes=[
            pltpu.VMEM((N, N), f32),
            pltpu.VMEM((N, N), f32),
            pltpu.VMEM((NB, N), f32),
            pltpu.VMEM((64, 128), f32),
            pltpu.VMEM((64, 128), f32),
            pltpu.VMEM((64, 128), f32),
            pltpu.VMEM((NB, N), f32),
            pltpu.VMEM((NB, N), f32),
            pltpu.VMEM((N, NB), f32),
        ],
        compiler_params=pltpu.CompilerParams(vmem_limit_bytes=40 << 20),
        name="panel_step",
    )(flags, mine, other, panel, trail, trail_other)


def on_device(panel, trail):
    plane = ("y", "x")
    z = lax.axis_index("z")
    member = lax.axis_index(plane)
    core = lax.axis_index("core")
    row = z * lax.axis_size(plane) + member
    trail_other = lax.ppermute(trail.reshape(512, N), "core", [(0, 1), (1, 0)])
    sent = jnp.where((row == 1) & (core == 0), trail[0, :, 0, :], panel[0]).reshape(16, 16, N)
    got = lax.all_to_all(sent, plane, 0, 0)
    shares = jnp.where(core == 0, got[:3:2, :8], got[:3:2, 8:])
    piece = jnp.concatenate([shares[0], got[1], shares[1]], 0)
    piece = jnp.where(z == 0, piece, 0.0)
    for pairs in Z_STEPS:
        piece = piece + lax.ppermute(piece, "z", pairs)
    mine = lax.all_to_all(jnp.broadcast_to(piece[None], (16, 32, N)), plane, 0, 0)
    other = lax.ppermute(mine, "core", [(0, 1), (1, 0)])
    flags = jnp.stack([row, core]).astype(jnp.int32)
    pf, up, nx = local_part(
        flags, mine, other, panel.reshape(512, N), trail.reshape(512, N), trail_other
    )
    return pf.reshape(2, N, N), up.reshape(2, N, 1, N), nx.reshape(2, N, 128)


def solution(mesh):
    grid = Mesh(mesh.devices.reshape(8, 4, 4, 2), ("z", "y", "x", "core"))
    rows = ("z", "y", "x")
    return jax.shard_map(
        on_device,
        mesh=grid,
        in_specs=(P(None, rows, None), P(None, rows, None, "core")),
        out_specs=(P(None, rows, None), P(None, rows, None, "core"), P(None, rows, "core")),
        check_vma=False,
    )
```

time: 80 us -> 71.7 us (0.90)
  Pallas kernels: 28.9 us -> 20.3 us
  starting transfers between devices: 26.6 us -> 28 us
    pallas_call x1, Pallas kernels: 28.9 us -> 20.3 us  [local_part(): pl.pallas_call(kernel, out_shape=[jax.ShapeDtypeStruct((512, N), f32), ja...]
    slice x3 -> x4, local copies, waits for them, and re-layouts: 1.92 us -> 1.85 us  [the longest x2 0.95 us: on_device(): trail[0, :, 0, :]]
where the time goes in v2:
time: 71.7 us; the launch traced here: 71.3 us
  starting transfers between devices  28 us (39%)
  Pallas kernels  20.3 us (28%)
  waiting for transfers between devices  17.3 us (24%)
  local copies, waits for them, and re-layouts  4.1 us (6%)
  other arithmetic  0.84 us (1%)
  between operations  0.76 us (1%)
    pallas_call x1, Pallas kernels, local_part(): pl.pallas_call(kernel, out_shape=[jax.ShapeDtypeStruct((512, N), f32), ja...  20.3 us
    ppermute x3, starting transfers between devices, on_device(): piece = piece + lax.ppermute(piece, 'z', pairs)  8.44 us
    all_to_all x1, starting transfers between devices, on_device(): got = lax.all_to_all(sent, plane, 0, 0)  7.57 us
    all_to_all x1, waiting for transfers between devices, on_device(): got = lax.all_to_all(sent, plane, 0, 0)  7.54 us
    all_to_all x1, waiting for transfers between devices, on_device(): lax.all_to_all(jnp.broadcast_to(piece[None], (16, 32, N)), plane, 0, 0)  5.31 us
    ppermute x1, starting transfers between devices, on_device(): other = lax.ppermute(mine, 'core', [(0, 1), (1, 0)])  4.64 us
    all_to_all x1, starting transfers between devices, on_device(): lax.all_to_all(jnp.broadcast_to(piece[None], (16, 32, N)), plane, 0, 0)  3.71 us
    ppermute x1, starting transfers between devices, on_device(): trail_other = lax.ppermute(trail.reshape(512, N), 'core', [(0, 1), (1, 0)])  3.62 us
  transfers between devices with their start and end apart: 7, of which 6 were waited for; matrix products, arithmetic and copies ran while one was open for 0% of the time, Pallas kernels for 0%

profile of v2, /device:TPU:1, one launch (start us, length us, event | category | flops | bytes accessed | tf_op | source)
XLA Modules:
  0.0 71.3 jit_solution(12940103445730236612)
XLA Ops:
  0.6 0.0 slice-start.1
  0.6 0.9 %slice-done.1 = f32[1,256,1,256]{3,2,1,0:T(1,128)S(1)} async-done(((f32[2,256,1,256]{3,2,1,0:T(1,128)}), f32[1,256,1,256]{3,2,1,0:T(1,128)S(1)}, s32[]{:S(2)}) %slice-start.1) | async-done | bytes 262168 | tf_op jit(solution)/shard_map/slice | solution.py:231
  1.6 0.0 slice-start
  1.6 0.9 %slice-done = f32[1,256,256]{2,1,0:T(8,128)S(1)} async-done(((f32[2,256,256]{2,1,0:T(8,128)}), f32[1,256,256]{2,1,0:T(8,128)S(1)}, s32[]{:S(2)}) %slice-start) | async-done | bytes 262168 | tf_op jit(solution)/shard_map/slice | solution.py:231
  2.5 0.7 %broadcast_select_fusion = f32[16,16,256]{2,1,0:T(8,128)} fusion(f32[16,16,256]{2,1,0:T(8,128)S(1)} %bitcast.20, f32[16,16,256]{2,1,0:T(8,128)S(1)} %bitcast.18, pred[]{:T(512)S(6)} %and.7), kind=kLoop, calls=%fused_computation | loop fusion | flops 65536 | bytes 786433 | tf_op jit(solution)/shard_map/jit(_where)/select_n | solution.py:231
  3.3 7.6 %all-to-all-start = ((f32[16,16,256]{2,1,0:T(8,128)}), f32[16,16,256]{2,1,0:T(8,128)S(1)}, u32[]{:S(2)}, u32[]{:S(2)}) async-start(f32[16,16,256]{2,1,0:T(8,128)} %broadcast_select_fusion), calls=%async_computation | async-start | bytes 524288 | tf_op jit(solution)/shard_map/all_to_all | solution.py:232
  10.9 7.5 %all-to-all-done = f32[16,16,256]{2,1,0:T(8,128)S(1)} async-done(((f32[16,16,256]{2,1,0:T(8,128)}), f32[16,16,256]{2,1,0:T(8,128)S(1)}, u32[]{:S(2)}, u32[]{:S(2)}) %all-to-all-start) | async-done | bytes 262176 | tf_op jit(solution)/shard_map/all_to_all | solution.py:232
  18.4 3.5 %collective-permute-start = (f32[32,256]{1,0:T(8,128)S(1)}, f32[32,256]{1,0:T(8,128)S(1)}, u32[]{:S(2)}, u32[]{:S(2)}) collective-permute-start(f32[32,256]{1,0:T(8,128)S(1)} %maximum_select_fusion), channel_id=1, source_target_pairs={{0,32},{1,33},{2,34},{3,35},{4,36},{5,37},{6,38},{7,39},{8,40},{9,... | collective-permute-start | bytes 98312 | tf_op jit(solution)/shard_map/ppermute | solution.py:237
  22.0 1.0 %collective-permute-done = f32[32,256]{1,0:T(8,128)S(1)} collective-permute-done((f32[32,256]{1,0:T(8,128)S(1)}, f32[32,256]{1,0:T(8,128)S(1)}, u32[]{:S(2)}, u32[]{:S(2)}) %collective-permute-start) | collective-permute-done | bytes 32800 | tf_op jit(solution)/shard_map/ppermute | solution.py:237
  23.0 3.6 %collective-permute-start.1 = (f32[32,256]{1,0:T(8,128)S(1)}, f32[32,256]{1,0:T(8,128)S(1)}, u32[]{:S(2)}, u32[]{:S(2)}) collective-permute-start(f32[32,256]{1,0:T(8,128)S(1)} %add.17), channel_id=1, source_target_pairs={{0,224},{32,64},{1,225},{33,65},{2,226},{34,66},{3,227},{35,67},{4... | collective-permute-start | bytes 98312 | tf_op jit(solution)/shard_map/ppermute | solution.py:237
  26.6 1.0 %collective-permute-done.1 = f32[32,256]{1,0:T(8,128)S(1)} collective-permute-done((f32[32,256]{1,0:T(8,128)S(1)}, f32[32,256]{1,0:T(8,128)S(1)}, u32[]{:S(2)}, u32[]{:S(2)}) %collective-permute-start.1) | collective-permute-done | bytes 32800 | tf_op jit(solution)/shard_map/ppermute | solution.py:237
  27.6 1.3 %collective-permute-start.2 = (f32[32,256]{1,0:T(8,128)S(1)}, f32[32,256]{1,0:T(8,128)S(1)}, u32[]{:S(2)}, u32[]{:S(2)}) collective-permute-start(f32[32,256]{1,0:T(8,128)S(1)} %add.18), channel_id=1, source_target_pairs={{0,160},{32,128},{64,96},{224,192},{1,161},{33,129},{65,97},{225,1... | collective-permute-start | bytes 98312 | tf_op jit(solution)/shard_map/ppermute | solution.py:237
  28.9 1.0 %collective-permute-done.2 = f32[32,256]{1,0:T(8,128)S(1)} collective-permute-done((f32[32,256]{1,0:T(8,128)S(1)}, f32[32,256]{1,0:T(8,128)S(1)}, u32[]{:S(2)}, u32[]{:S(2)}) %collective-permute-start.2) | collective-permute-done | bytes 32800 | tf_op jit(solution)/shard_map/ppermute | solution.py:237
  29.9 0.8 %broadcast_in_dim.11 = f32[16,32,256]{2,1,0:T(8,128)} broadcast(f32[32,256]{1,0:T(8,128)S(1)} %add.19), dimensions={1,2} | broadcast | bytes 557056 | tf_op jit(solution)/shard_map/broadcast_in_dim | solution.py:238
  30.8 0.0 copy-start.1
  30.8 3.7 %all-to-all-start.1 = ((f32[16,32,256]{2,1,0:T(8,128)}), f32[16,32,256]{2,1,0:T(8,128)S(1)}, u32[]{:S(2)}, u32[]{:S(2)}) async-start(f32[16,32,256]{2,1,0:T(8,128)} %broadcast_in_dim.11), calls=%async_computation.1 | async-start | bytes 1048576 | tf_op jit(solution)/shard_map/all_to_all | solution.py:238
  34.5 0.0 copy-done.1
  34.5 0.0 copy-start
  34.6 3.6 %collective-permute-start.4 = (f32[512,256]{1,0:T(8,128)S(1)}, f32[512,256]{1,0:T(8,128)S(1)}, u32[]{:S(2)}, u32[]{:S(2)}) collective-permute-start(f32[512,256]{1,0:T(8,128)S(1)} %bitcast.15), channel_id=1, source_target_pairs={{0,1},{1,0},{2,3},{3,2},{4,5},{5,4},{6,7},{7,6},{8,9},{9,8},{10,11... | collective-permute-start | bytes 1572872 | tf_op jit(solution)/shard_map/ppermute | solution.py:230
  38.2 5.3 %all-to-all-done.1.mine = f32[16,32,256]{2,1,0:T(8,128)S(1)} async-done(((f32[16,32,256]{2,1,0:T(8,128)}), f32[16,32,256]{2,1,0:T(8,128)S(1)}, u32[]{:S(2)}, u32[]{:S(2)}) %all-to-all-start.1) | async-done | bytes 524320 | tf_op jit(solution)/shard_map/all_to_all | solution.py:238
  43.5 4.6 %collective-permute-start.3 = (f32[16,32,256]{2,1,0:T(8,128)S(1)}, f32[16,32,256]{2,1,0:T(8,128)S(1)}, u32[]{:S(2)}, u32[]{:S(2)}) collective-permute-start(f32[16,32,256]{2,1,0:T(8,128)S(1)} %all-to-all-done.1.mine), channel_id=1, source_target_pairs={{0,1},{1,0},{2,3},{3,2},{4,5},{5,4},{6,7},{7,6},{8,9},{9,8},{10,11... | collective-permute-start | bytes 1572872 | tf_op jit(solution)/shard_map/ppermute | solution.py:239
  48.1 0.1 pad_add_fusion.flags
  48.2 0.0 collective-permute-done.4.trail_other
  48.2 1.5 %collective-permute-done.3.other = f32[16,32,256]{2,1,0:T(8,128)S(1)} collective-permute-done((f32[16,32,256]{2,1,0:T(8,128)S(1)}, f32[16,32,256]{2,1,0:T(8,128)S(1)}, u32[]{:S(2)}, u32[]{:S(2)}) %collective-permute-start.3) | collective-permute-done | bytes 524320 | tf_op jit(solution)/shard_map/ppermute | solution.py:239
  49.7 0.0 copy-done
  49.7 20.3 %panel_step.1 = (f32[512,256]{1,0:T(8,128)}, f32[512,256]{1,0:T(8,128)S(1)}, f32[512,128]{1,0:T(8,128)}) custom-call(s32[2]{0:T(128)S(1)} %pad_add_fusion.flags, f32[16,32,256]{2,1,0:T(8,128)S(1)} %all-to-all-done.1.mine, f32[16,32,256]{2,1,0:T(8,128)S(1)} %collective-permute-done.3.other, f32[512,256]{1,0:T(8,128)S(1)} %bitcast.17, ...), custom_call_target="tpu_custom_call" | custom-call | tf_op jit(solution)/shard_map/panel_step/pallas_call | solution.py:199
  70.0 1.3 %copy.5 = f32[2,256,1,256]{3,2,1,0:T(1,128)} copy(f32[2,256,1,256]{3,1,0,2:T(8,128)S(1)} %bitcast.19) | data formatting | bytes 1048576
  (9 shorter events, 0.1 us)
Async XLA Ops:
  0.6 1.0 %slice-start.1 = ((f32[2,256,1,256]{3,2,1,0:T(1,128)}), f32[1,256,1,256]{3,2,1,0:T(1,128)S(1)}, s32[]{:S(2)}) async-start(f32[2,256,1,256]{3,2,1,0:T(1,128)} %param.3), calls=%async_computation.3 | async-start | bytes 524288 | tf_op jit(solution)/shard_map/slice | solution.py:231
  1.6 0.9 %slice-start = ((f32[2,256,256]{2,1,0:T(8,128)}), f32[1,256,256]{2,1,0:T(8,128)S(1)}, s32[]{:S(2)}) async-start(f32[2,256,256]{2,1,0:T(8,128)} %param.2), calls=%async_computation.2 | async-start | bytes 524288 | tf_op jit(solution)/shard_map/slice | solution.py:231
  3.3 15.1 %all-to-all-start = ((f32[16,16,256]{2,1,0:T(8,128)}), f32[16,16,256]{2,1,0:T(8,128)S(1)}, u32[]{:S(2)}, u32[]{:S(2)}) async-start(f32[16,16,256]{2,1,0:T(8,128)} %broadcast_select_fusion), calls=%async_computation | async-start | bytes 524288 | tf_op jit(solution)/shard_map/all_to_all | solution.py:232
  18.4 4.6 %collective-permute-start = (f32[32,256]{1,0:T(8,128)S(1)}, f32[32,256]{1,0:T(8,128)S(1)}, u32[]{:S(2)}, u32[]{:S(2)}) collective-permute-start(f32[32,256]{1,0:T(8,128)S(1)} %maximum_select_fusion), channel_id=1, source_target_pairs={{0,32},{1,33},{2,34},{3,35},{4,36},{5,37},{6,38},{7,39},{8,40},{9,... | collective-permute-start | bytes 98312 | tf_op jit(solution)/shard_map/ppermute | solution.py:237
  23.0 4.6 %collective-permute-start.1 = (f32[32,256]{1,0:T(8,128)S(1)}, f32[32,256]{1,0:T(8,128)S(1)}, u32[]{:S(2)}, u32[]{:S(2)}) collective-permute-start(f32[32,256]{1,0:T(8,128)S(1)} %add.17), channel_id=1, source_target_pairs={{0,224},{32,64},{1,225},{33,65},{2,226},{34,66},{3,227},{35,67},{4... | collective-permute-start | bytes 98312 | tf_op jit(solution)/shard_map/ppermute | solution.py:237
  27.6 2.3 %collective-permute-start.2 = (f32[32,256]{1,0:T(8,128)S(1)}, f32[32,256]{1,0:T(8,128)S(1)}, u32[]{:S(2)}, u32[]{:S(2)}) collective-permute-start(f32[32,256]{1,0:T(8,128)S(1)} %add.18), channel_id=1, source_target_pairs={{0,160},{32,128},{64,96},{224,192},{1,161},{33,129},{65,97},{225,1... | collective-permute-start | bytes 98312 | tf_op jit(solution)/shard_map/ppermute | solution.py:237
  30.8 3.7 %copy-start.1 = (f32[2,256,1,256]{3,2,1,0:T(1,128)S(1)}, f32[2,256,1,256]{3,2,1,0:T(1,128)}, u32[]{:S(2)}) copy-start(f32[2,256,1,256]{3,2,1,0:T(1,128)} %param.3) | copy-start | bytes 1572868
  30.8 12.7 %all-to-all-start.1 = ((f32[16,32,256]{2,1,0:T(8,128)}), f32[16,32,256]{2,1,0:T(8,128)S(1)}, u32[]{:S(2)}, u32[]{:S(2)}) async-start(f32[16,32,256]{2,1,0:T(8,128)} %broadcast_in_dim.11), calls=%async_computation.1 | async-start | bytes 1048576 | tf_op jit(solution)/shard_map/all_to_all | solution.py:238
  34.5 15.2 %copy-start = (f32[2,256,256]{2,1,0:T(8,128)S(1)}, f32[2,256,256]{2,1,0:T(8,128)}, u32[]{:S(2)}) copy-start(f32[2,256,256]{2,1,0:T(8,128)} %param.2) | copy-start | bytes 1572868
  34.6 13.6 %collective-permute-start.4 = (f32[512,256]{1,0:T(8,128)S(1)}, f32[512,256]{1,0:T(8,128)S(1)}, u32[]{:S(2)}, u32[]{:S(2)}) collective-permute-start(f32[512,256]{1,0:T(8,128)S(1)} %bitcast.15), channel_id=1, source_target_pairs={{0,1},{1,0},{2,3},{3,2},{4,5},{5,4},{6,7},{7,6},{8,9},{9,8},{10,11... | collective-permute-start | bytes 1572872 | tf_op jit(solution)/shard_map/ppermute | solution.py:230
  43.5 6.2 %collective-permute-start.3 = (f32[16,32,256]{2,1,0:T(8,128)S(1)}, f32[16,32,256]{2,1,0:T(8,128)S(1)}, u32[]{:S(2)}, u32[]{:S(2)}) collective-permute-start(f32[16,32,256]{2,1,0:T(8,128)S(1)} %all-to-all-done.1.mine), channel_id=1, source_target_pairs={{0,1},{1,0},{2,3},{3,2},{4,5},{5,4},{6,7},{7,6},{8,9},{9,8},{10,11... | collective-permute-start | bytes 1572872 | tf_op jit(solution)/shard_map/ppermute | solution.py:239

commit v3 on v2

--- a/solution.py
+++ b/solution.py
@@ -32,18 +32,20 @@
 def dot_nt3(a, b):
     a_hi, a_lo = split(a)
     b_hi, b_lo = b
-
-    def part(u, v):
-        return lax.dot_general(u, v, (((1,), (1,)), ((), ())), preferred_element_type=jnp.float32)
-
-    return part(a_hi, b_hi) + (part(a_hi, b_lo) + part(a_lo, b_hi))
-
-
-def dot_nn(a, b):
     return lax.dot_general(
-        a, b, (((1,), (0,)), ((), ())),
-        precision=lax.Precision.HIGHEST, preferred_element_type=jnp.float32,
-    )
+        jnp.concatenate([a_hi, a_hi, a_lo], 1), jnp.concatenate([b_hi, b_lo, b_hi], 1),
+        (((1,), (1,)), ((), ())), preferred_element_type=jnp.float32,
+    )
+
+
+def three_parts(a):
+    one = a.astype(jnp.bfloat16).astype(jnp.float32)
+    two = (a - one).astype(jnp.bfloat16).astype(jnp.float32)
+    return one, two, a - one - two
+
+
+def dot_bf16(a, b):
+    return lax.dot_general(a, b, (((1,), (0,)), ((), ())), preferred_element_type=jnp.float32)
 
 
 def spread_row(ref, i, h):
@@ -75,21 +77,20 @@
         in_block = (lane >= r0) & (lane < r0 + NB)
         xb[...] = jnp.where(in_block, jnp.where(lane - r0 == sub, 1.0, 0.0), rows)
         z_old = zb[...]
-        tt[lo:, :] = jnp.where(lane[:, lo:] >= r0 + NB, z_old[:, lo:], 0.0).T
+        one, two, three = three_parts(z_old)
+        left = jnp.concatenate([one, one, two, one, two, three], 0)
+        right = jnp.concatenate([one, two, one, three, two, one], 0).astype(jnp.bfloat16)
+        tt[lo:, :] = left[:, lo:].T.astype(jnp.bfloat16)
         gone = (lane >= r0 - NB) & (lane < r0)
-        nxt = jnp.where(gone, 0.0, w[pl.ds(n0, NB), :]) - dot_nn(tt[pl.ds(n0, NB), :], z_old)
+        nxt = jnp.where(gone, 0.0, w[pl.ds(n0, NB), :]) - dot_bf16(tt[pl.ds(n0, NB), :], right)
         for j in range(8):
             v[j] += [column(nxt[:8, lo:lo + 128], j), column(nxt[8:, lo:lo + 128], j)]
         c = [[column(nxt[8 * n:8 * n + 8, lo:lo + 128], 8 + j) for n in range(2)] for j in range(8)]
         nxt = jnp.where(in_block, 0.0, nxt)
         acc = [[nxt[8 * n:8 * n + 8, 128 * h:128 * h + 128] for h in range(2)] for n in range(2)]
         lane_r = lax.broadcasted_iota(jnp.int32, (N - lo, N), 1)
-        row_r = lax.broadcasted_iota(jnp.int32, (N - lo, N), 0) + lo
-        old = w[lo:, :]
         gone_r = (lane_r >= r0 - NB) & (lane_r < r0)
-        w[lo:, :] = jnp.where(
-            row_r >= r0 + NB, jnp.where(gone_r, 0.0, old) - dot_nn(tt[lo:, :], z_old), old
-        )
+        w[lo:, :] = jnp.where(gone_r, 0.0, w[lo:, :]) - dot_bf16(tt[lo:, :], right)
         y_all = []
         for g in range(2):
             if g == 0:
@@ -144,6 +145,9 @@
 
 
 def kernel(flags, mine, other, panel, trail, trail_other, pf, up, nx, w, inv, *work):
+    *work, panel_in, solved_out, up_out, nx_out, sems = work
+    fetch = pltpu.make_async_copy(panel, panel_in, sems.at[0])
+    fetch.start()
     row, core = flags[0], flags[1]
     is0 = core == 0
     lane_all = lax.broadcasted_iota(jnp.int32, (N, N), 1)
@@ -168,20 +172,29 @@
     inv1 = split(inv1)
     below_own = split(jnp.where(is0, below1, dot_nt3(block2, inv1)))
     below1 = split(below1)
+    fetch.wait()
+    copies = []
     for slot in range(2):
         rows = pl.ds(slot * N, N)
-        solved = dot_nt3(panel[rows, :], inv1)
+        solved = dot_nt3(panel_in[rows, :], inv1)
         carried = solved
         if slot == 0:
             first = row == 0
             solved = jnp.where(first & ~low, 0.0, solved)
             carried = jnp.where(first, 0.0, solved)
-        pf[rows, :] = solved
-        up[rows, :] = trail[rows, :] - dot_nt3(carried, below_own)
-        lead = jnp.where(is0, trail[rows, :], trail_other[rows, :]) - dot_nt3(carried, below1)
+        solved_out[rows, :] = solved
+        base = trail[rows, :]
+        updated = base - dot_nt3(carried, below_own)
+        for h in range(2):
+            up_out[pl.ds(512 * slot + h, N, stride=2), :] = updated[:, 128 * h:128 * h + 128]
+        lead = jnp.where(is0, base, trail_other[rows, :]) - dot_nt3(carried, below1)
         if slot == 0:
             lead = jnp.where(row == 1, corner, lead)
         trail_other[rows, :] = lead
+    copies.append(pltpu.make_async_copy(solved_out, pf, sems.at[1]))
+    copies.append(pltpu.make_async_copy(up_out, up, sems.at[2]))
+    for copy in copies:
+        copy.start()
     factor_inverse(w, inv, *work)
     half = split(inv[pl.ds(pl.multiple_of(core * 128, 128), 128), :])
     low_half = lane_all[:, :128] + core * 128 <= row_all[:, :128]
@@ -190,21 +203,27 @@
         solved = dot_nt3(trail_other[rows, :], half)
         if slot == 0:
             solved = jnp.where((row == 0) | ((row == 1) & ~low_half), 0.0, solved)
-        nx[rows, :] = solved
+        nx_out[rows, :] = solved
+        copy = pltpu.make_async_copy(nx_out.at[rows, :], nx.at[rows, :], sems.at[3 + slot])
+        copy.start()
+        copies.append(copy)
+    for copy in copies:
+        copy.wait()
 
 
 def local_part(flags, mine, other, panel, trail, trail_other):
     vmem = pl.BlockSpec(memory_space=pltpu.VMEM)
+    anywhere = pl.BlockSpec(memory_space=pl.ANY)
     f32 = jnp.float32
     return pl.pallas_call(
         kernel,
         out_shape=[
             jax.ShapeDtypeStruct((512, N), f32),
-            jax.ShapeDtypeStruct((512, N), f32),
+            jax.ShapeDtypeStruct((1024, 128), f32),
             jax.ShapeDtypeStruct((512, 128), f32),
         ],
-        in_specs=[pl.BlockSpec(memory_space=pltpu.SMEM)] + [vmem] * 5,
-        out_specs=[vmem] * 3,
+        in_specs=[pl.BlockSpec(memory_space=pltpu.SMEM), vmem, vmem, anywhere, vmem, vmem],
+        out_specs=[anywhere] * 3,
         scratch_shapes=[
             pltpu.VMEM((N, N), f32),
             pltpu.VMEM((N, N), f32),
@@ -214,7 +233,12 @@
             pltpu.VMEM((64, 128), f32),
             pltpu.VMEM((NB, N), f32),
             pltpu.VMEM((NB, N), f32),
-            pltpu.VMEM((N, NB), f32),
+            pltpu.VMEM((N, 6 * NB), jnp.bfloat16),
+            pltpu.VMEM((512, N), f32),
+            pltpu.VMEM((512, N), f32),
+            pltpu.VMEM((1024, 128), f32),
+            pltpu.VMEM((512, 128), f32),
+            pltpu.SemaphoreType.DMA((5,)),
         ],
         compiler_params=pltpu.CompilerParams(vmem_limit_bytes=40 << 20),
         name="panel_step",

time: 71.7 us -> 68.3 us (0.953)
  Pallas kernels: 20.3 us -> 18.2 us
  local copies, waits for them, and re-layouts: 4.1 us -> 2.77 us
    pallas_call x1, Pallas kernels: 20.3 us -> 18.2 us  [local_part(): pl.pallas_call(kernel, out_shape=[jax.ShapeDtypeStruct((512, N), f32), ja...]
    unnamed x7 -> x6, local copies, waits for them, and re-layouts: 1.4 us -> 0.06 us
where the time goes in v3:
time: 68.3 us; the launch traced here: 67.9 us
  starting transfers between devices  28 us (41%)
  Pallas kernels  18.2 us (27%)
  waiting for transfers between devices  17.3 us (25%)
  local copies, waits for them, and re-layouts  2.77 us (4%)
  other arithmetic  0.84 us (1%)
  between operations  0.76 us (1%)
    pallas_call x1, Pallas kernels, local_part(): pl.pallas_call(kernel, out_shape=[jax.ShapeDtypeStruct((512, N), f32), ja...  18.2 us
    ppermute x3, starting transfers between devices, on_device(): piece = piece + lax.ppermute(piece, 'z', pairs)  8.44 us
    all_to_all x1, starting transfers between devices, on_device(): got = lax.all_to_all(sent, plane, 0, 0)  7.57 us
    all_to_all x1, waiting for transfers between devices, on_device(): got = lax.all_to_all(sent, plane, 0, 0)  7.54 us
    all_to_all x1, waiting for transfers between devices, on_device(): lax.all_to_all(jnp.broadcast_to(piece[None], (16, 32, N)), plane, 0, 0)  5.31 us
    ppermute x1, starting transfers between devices, on_device(): other = lax.ppermute(mine, 'core', [(0, 1), (1, 0)])  4.64 us
    all_to_all x1, starting transfers between devices, on_device(): lax.all_to_all(jnp.broadcast_to(piece[None], (16, 32, N)), plane, 0, 0)  3.71 us
    ppermute x1, starting transfers between devices, on_device(): trail_other = lax.ppermute(trail.reshape(512, N), 'core', [(0, 1), (1, 0)])  3.62 us
  transfers between devices with their start and end apart: 7, of which 6 were waited for; matrix products, arithmetic and copies ran while one was open for 0% of the time, Pallas kernels for 0%

profile of v3, /device:TPU:1, one launch (start us, length us, event | category | flops | bytes accessed | tf_op | source)
XLA Modules:
  0.0 67.9 jit_solution(12162018151574635500)
XLA Ops:
  0.6 0.0 slice-start.1
  0.6 0.9 %slice-done.1 = f32[1,256,1,256]{3,2,1,0:T(1,128)S(1)} async-done(((f32[2,256,1,256]{3,2,1,0:T(1,128)}), f32[1,256,1,256]{3,2,1,0:T(1,128)S(1)}, s32[]{:S(2)}) %slice-start.1) | async-done | bytes 262168 | tf_op jit(solution)/shard_map/slice | solution.py:255
  1.6 0.0 slice-start
  1.6 0.9 %slice-done = f32[1,256,256]{2,1,0:T(8,128)S(1)} async-done(((f32[2,256,256]{2,1,0:T(8,128)}), f32[1,256,256]{2,1,0:T(8,128)S(1)}, s32[]{:S(2)}) %slice-start) | async-done | bytes 262168 | tf_op jit(solution)/shard_map/slice | solution.py:255
  2.5 0.7 %broadcast_select_fusion = f32[16,16,256]{2,1,0:T(8,128)} fusion(f32[16,16,256]{2,1,0:T(8,128)S(1)} %bitcast.19, f32[16,16,256]{2,1,0:T(8,128)S(1)} %bitcast.18, pred[]{:T(512)S(6)} %and.7), kind=kLoop, calls=%fused_computation | loop fusion | flops 65536 | bytes 786433 | tf_op jit(solution)/shard_map/jit(_where)/select_n | solution.py:255
  3.3 7.6 %all-to-all-start = ((f32[16,16,256]{2,1,0:T(8,128)}), f32[16,16,256]{2,1,0:T(8,128)S(1)}, u32[]{:S(2)}, u32[]{:S(2)}) async-start(f32[16,16,256]{2,1,0:T(8,128)} %broadcast_select_fusion), calls=%async_computation | async-start | bytes 524288 | tf_op jit(solution)/shard_map/all_to_all | solution.py:256
  10.9 7.5 %all-to-all-done = f32[16,16,256]{2,1,0:T(8,128)S(1)} async-done(((f32[16,16,256]{2,1,0:T(8,128)}), f32[16,16,256]{2,1,0:T(8,128)S(1)}, u32[]{:S(2)}, u32[]{:S(2)}) %all-to-all-start) | async-done | bytes 262176 | tf_op jit(solution)/shard_map/all_to_all | solution.py:256
  18.4 3.5 %collective-permute-start = (f32[32,256]{1,0:T(8,128)S(1)}, f32[32,256]{1,0:T(8,128)S(1)}, u32[]{:S(2)}, u32[]{:S(2)}) collective-permute-start(f32[32,256]{1,0:T(8,128)S(1)} %maximum_select_fusion), channel_id=1, source_target_pairs={{0,32},{1,33},{2,34},{3,35},{4,36},{5,37},{6,38},{7,39},{8,40},{9,... | collective-permute-start | bytes 98312 | tf_op jit(solution)/shard_map/ppermute | solution.py:261
  22.0 1.0 %collective-permute-done = f32[32,256]{1,0:T(8,128)S(1)} collective-permute-done((f32[32,256]{1,0:T(8,128)S(1)}, f32[32,256]{1,0:T(8,128)S(1)}, u32[]{:S(2)}, u32[]{:S(2)}) %collective-permute-start) | collective-permute-done | bytes 32800 | tf_op jit(solution)/shard_map/ppermute | solution.py:261
  23.0 3.6 %collective-permute-start.1 = (f32[32,256]{1,0:T(8,128)S(1)}, f32[32,256]{1,0:T(8,128)S(1)}, u32[]{:S(2)}, u32[]{:S(2)}) collective-permute-start(f32[32,256]{1,0:T(8,128)S(1)} %add.17), channel_id=1, source_target_pairs={{0,224},{32,64},{1,225},{33,65},{2,226},{34,66},{3,227},{35,67},{4... | collective-permute-start | bytes 98312 | tf_op jit(solution)/shard_map/ppermute | solution.py:261
  26.6 1.0 %collective-permute-done.1 = f32[32,256]{1,0:T(8,128)S(1)} collective-permute-done((f32[32,256]{1,0:T(8,128)S(1)}, f32[32,256]{1,0:T(8,128)S(1)}, u32[]{:S(2)}, u32[]{:S(2)}) %collective-permute-start.1) | collective-permute-done | bytes 32800 | tf_op jit(solution)/shard_map/ppermute | solution.py:261
  27.6 1.3 %collective-permute-start.2 = (f32[32,256]{1,0:T(8,128)S(1)}, f32[32,256]{1,0:T(8,128)S(1)}, u32[]{:S(2)}, u32[]{:S(2)}) collective-permute-start(f32[32,256]{1,0:T(8,128)S(1)} %add.18), channel_id=1, source_target_pairs={{0,160},{32,128},{64,96},{224,192},{1,161},{33,129},{65,97},{225,1... | collective-permute-start | bytes 98312 | tf_op jit(solution)/shard_map/ppermute | solution.py:261
  28.9 1.0 %collective-permute-done.2 = f32[32,256]{1,0:T(8,128)S(1)} collective-permute-done((f32[32,256]{1,0:T(8,128)S(1)}, f32[32,256]{1,0:T(8,128)S(1)}, u32[]{:S(2)}, u32[]{:S(2)}) %collective-permute-start.2) | collective-permute-done | bytes 32800 | tf_op jit(solution)/shard_map/ppermute | solution.py:261
  29.9 0.8 %broadcast_in_dim.11 = f32[16,32,256]{2,1,0:T(8,128)} broadcast(f32[32,256]{1,0:T(8,128)S(1)} %add.19), dimensions={1,2} | broadcast | bytes 557056 | tf_op jit(solution)/shard_map/broadcast_in_dim | solution.py:262
  30.8 0.0 copy-start.1
  30.8 3.7 %all-to-all-start.1 = ((f32[16,32,256]{2,1,0:T(8,128)}), f32[16,32,256]{2,1,0:T(8,128)S(1)}, u32[]{:S(2)}, u32[]{:S(2)}) async-start(f32[16,32,256]{2,1,0:T(8,128)} %broadcast_in_dim.11), calls=%async_computation.1 | async-start | bytes 1048576 | tf_op jit(solution)/shard_map/all_to_all | solution.py:262
  34.5 0.0 copy-done.1
  34.5 0.0 copy-start
  34.6 3.6 %collective-permute-start.4 = (f32[512,256]{1,0:T(8,128)S(1)}, f32[512,256]{1,0:T(8,128)S(1)}, u32[]{:S(2)}, u32[]{:S(2)}) collective-permute-start(f32[512,256]{1,0:T(8,128)S(1)} %bitcast.15), channel_id=1, source_target_pairs={{0,1},{1,0},{2,3},{3,2},{4,5},{5,4},{6,7},{7,6},{8,9},{9,8},{10,11... | collective-permute-start | bytes 1572872 | tf_op jit(solution)/shard_map/ppermute | solution.py:254
  38.2 5.3 %all-to-all-done.1.mine = f32[16,32,256]{2,1,0:T(8,128)S(1)} async-done(((f32[16,32,256]{2,1,0:T(8,128)}), f32[16,32,256]{2,1,0:T(8,128)S(1)}, u32[]{:S(2)}, u32[]{:S(2)}) %all-to-all-start.1) | async-done | bytes 524320 | tf_op jit(solution)/shard_map/all_to_all | solution.py:262
  43.5 4.6 %collective-permute-start.3 = (f32[16,32,256]{2,1,0:T(8,128)S(1)}, f32[16,32,256]{2,1,0:T(8,128)S(1)}, u32[]{:S(2)}, u32[]{:S(2)}) collective-permute-start(f32[16,32,256]{2,1,0:T(8,128)S(1)} %all-to-all-done.1.mine), channel_id=1, source_target_pairs={{0,1},{1,0},{2,3},{3,2},{4,5},{5,4},{6,7},{7,6},{8,9},{9,8},{10,11... | collective-permute-start | bytes 1572872 | tf_op jit(solution)/shard_map/ppermute | solution.py:263
  48.1 0.1 pad_add_fusion.flags
  48.2 0.0 collective-permute-done.4.trail_other
  48.2 1.5 %collective-permute-done.3.other = f32[16,32,256]{2,1,0:T(8,128)S(1)} collective-permute-done((f32[16,32,256]{2,1,0:T(8,128)S(1)}, f32[16,32,256]{2,1,0:T(8,128)S(1)}, u32[]{:S(2)}, u32[]{:S(2)}) %collective-permute-start.3) | collective-permute-done | bytes 524320 | tf_op jit(solution)/shard_map/ppermute | solution.py:263
  49.7 0.0 copy-done
  49.7 18.2 %panel_step.1 = (f32[512,256]{1,0:T(8,128)}, f32[1024,128]{1,0:T(8,128)}, f32[512,128]{1,0:T(8,128)}) custom-call(s32[2]{0:T(128)S(1)} %pad_add_fusion.flags, f32[16,32,256]{2,1,0:T(8,128)S(1)} %all-to-all-done.1.mine, f32[16,32,256]{2,1,0:T(8,128)S(1)} %collective-permute-done.3.other, f32[512,256]{1,0:T(8,128)S(1)} %bitcast.17, f32[512,256]{1,0:T(8,128)S(1)} %bitcast.16, ...), custom_call_target="tpu_custom_call" | custom-call | tf_op jit(solution)/shard_map/panel_step/pallas_call | solution.py:218
  (9 shorter events, 0.1 us)
Async XLA Ops:
  0.6 1.0 %slice-start.1 = ((f32[2,256,1,256]{3,2,1,0:T(1,128)}), f32[1,256,1,256]{3,2,1,0:T(1,128)S(1)}, s32[]{:S(2)}) async-start(f32[2,256,1,256]{3,2,1,0:T(1,128)} %param.3), calls=%async_computation.3 | async-start | bytes 524288 | tf_op jit(solution)/shard_map/slice | solution.py:255
  1.6 0.9 %slice-start = ((f32[2,256,256]{2,1,0:T(8,128)}), f32[1,256,256]{2,1,0:T(8,128)S(1)}, s32[]{:S(2)}) async-start(f32[2,256,256]{2,1,0:T(8,128)} %param.2), calls=%async_computation.2 | async-start | bytes 524288 | tf_op jit(solution)/shard_map/slice | solution.py:255
  3.3 15.1 %all-to-all-start = ((f32[16,16,256]{2,1,0:T(8,128)}), f32[16,16,256]{2,1,0:T(8,128)S(1)}, u32[]{:S(2)}, u32[]{:S(2)}) async-start(f32[16,16,256]{2,1,0:T(8,128)} %broadcast_select_fusion), calls=%async_computation | async-start | bytes 524288 | tf_op jit(solution)/shard_map/all_to_all | solution.py:256
  18.4 4.6 %collective-permute-start = (f32[32,256]{1,0:T(8,128)S(1)}, f32[32,256]{1,0:T(8,128)S(1)}, u32[]{:S(2)}, u32[]{:S(2)}) collective-permute-start(f32[32,256]{1,0:T(8,128)S(1)} %maximum_select_fusion), channel_id=1, source_target_pairs={{0,32},{1,33},{2,34},{3,35},{4,36},{5,37},{6,38},{7,39},{8,40},{9,... | collective-permute-start | bytes 98312 | tf_op jit(solution)/shard_map/ppermute | solution.py:261
  23.0 4.6 %collective-permute-start.1 = (f32[32,256]{1,0:T(8,128)S(1)}, f32[32,256]{1,0:T(8,128)S(1)}, u32[]{:S(2)}, u32[]{:S(2)}) collective-permute-start(f32[32,256]{1,0:T(8,128)S(1)} %add.17), channel_id=1, source_target_pairs={{0,224},{32,64},{1,225},{33,65},{2,226},{34,66},{3,227},{35,67},{4... | collective-permute-start | bytes 98312 | tf_op jit(solution)/shard_map/ppermute | solution.py:261
  27.6 2.3 %collective-permute-start.2 = (f32[32,256]{1,0:T(8,128)S(1)}, f32[32,256]{1,0:T(8,128)S(1)}, u32[]{:S(2)}, u32[]{:S(2)}) collective-permute-start(f32[32,256]{1,0:T(8,128)S(1)} %add.18), channel_id=1, source_target_pairs={{0,160},{32,128},{64,96},{224,192},{1,161},{33,129},{65,97},{225,1... | collective-permute-start | bytes 98312 | tf_op jit(solution)/shard_map/ppermute | solution.py:261
  30.8 3.7 %copy-start.1 = (f32[2,256,1,256]{3,2,1,0:T(1,128)S(1)}, f32[2,256,1,256]{3,2,1,0:T(1,128)}, u32[]{:S(2)}) copy-start(f32[2,256,1,256]{3,2,1,0:T(1,128)} %param.3) | copy-start | bytes 1572868
  30.8 12.7 %all-to-all-start.1 = ((f32[16,32,256]{2,1,0:T(8,128)}), f32[16,32,256]{2,1,0:T(8,128)S(1)}, u32[]{:S(2)}, u32[]{:S(2)}) async-start(f32[16,32,256]{2,1,0:T(8,128)} %broadcast_in_dim.11), calls=%async_computation.1 | async-start | bytes 1048576 | tf_op jit(solution)/shard_map/all_to_all | solution.py:262
  34.5 15.2 %copy-start = (f32[2,256,256]{2,1,0:T(8,128)S(1)}, f32[2,256,256]{2,1,0:T(8,128)}, u32[]{:S(2)}) copy-start(f32[2,256,256]{2,1,0:T(8,128)} %param.2) | copy-start | bytes 1572868
  34.6 13.6 %collective-permute-start.4 = (f32[512,256]{1,0:T(8,128)S(1)}, f32[512,256]{1,0:T(8,128)S(1)}, u32[]{:S(2)}, u32[]{:S(2)}) collective-permute-start(f32[512,256]{1,0:T(8,128)S(1)} %bitcast.15), channel_id=1, source_target_pairs={{0,1},{1,0},{2,3},{3,2},{4,5},{5,4},{6,7},{7,6},{8,9},{9,8},{10,11... | collective-permute-start | bytes 1572872 | tf_op jit(solution)/shard_map/ppermute | solution.py:254
  43.5 6.2 %collective-permute-start.3 = (f32[16,32,256]{2,1,0:T(8,128)S(1)}, f32[16,32,256]{2,1,0:T(8,128)S(1)}, u32[]{:S(2)}, u32[]{:S(2)}) collective-permute-start(f32[16,32,256]{2,1,0:T(8,128)S(1)} %all-to-all-done.1.mine), channel_id=1, source_target_pairs={{0,1},{1,0},{2,3},{3,2},{4,5},{5,4},{6,7},{7,6},{8,9},{9,8},{10,11... | collective-permute-start | bytes 1572872 | tf_op jit(solution)/shard_map/ppermute | solution.py:263

commit v4 on v3

--- a/solution.py
+++ b/solution.py
@@ -17,13 +17,6 @@
 )
 
 
-def dot_nt(a, b):
-    return lax.dot_general(
-        a, b, (((1,), (1,)), ((), ())),
-        precision=lax.Precision.HIGHEST, preferred_element_type=jnp.float32,
-    )
-
-
 def split(a):
     high = a.astype(jnp.bfloat16)
     return high, (a - high.astype(jnp.float32)).astype(jnp.bfloat16)
@@ -42,6 +35,17 @@
     one = a.astype(jnp.bfloat16).astype(jnp.float32)
     two = (a - one).astype(jnp.bfloat16).astype(jnp.float32)
     return one, two, a - one - two
+
+
+def stack_six(a, b):
+    a1, a2, a3 = [t.astype(jnp.bfloat16) for t in three_parts(a)]
+    b1, b2, b3 = [t.astype(jnp.bfloat16) for t in three_parts(b)]
+    return jnp.concatenate([a1, a1, a2, a1, a2, a3], 1), jnp.concatenate([b1, b2, b1, b3, b2, b1], 1)
+
+
+def dot_nt6(a, b):
+    a, b = stack_six(a, b)
+    return lax.dot_general(a, b, (((1,), (1,)), ((), ())), preferred_element_type=jnp.float32)
 
 
 def dot_bf16(a, b):
@@ -88,10 +92,12 @@
         c = [[column(nxt[8 * n:8 * n + 8, lo:lo + 128], 8 + j) for n in range(2)] for j in range(8)]
         nxt = jnp.where(in_block, 0.0, nxt)
         acc = [[nxt[8 * n:8 * n + 8, 128 * h:128 * h + 128] for h in range(2)] for n in range(2)]
-        lane_r = lax.broadcasted_iota(jnp.int32, (N - lo, N), 1)
+        lane_r = lax.broadcasted_iota(jnp.int32, (N - lo, 128), 1) + lo
         gone_r = (lane_r >= r0 - NB) & (lane_r < r0)
-        w[lo:, :] = jnp.where(gone_r, 0.0, w[lo:, :]) - dot_bf16(tt[lo:, :], right)
-        y_all = []
+        late = dot_bf16(tt[lo:, :], right)
+        w[lo:, lo:lo + 128] = jnp.where(gone_r, 0.0, w[lo:, lo:lo + 128]) - late[:, lo:lo + 128]
+        w[lo:, 128 - lo:256 - lo] = w[lo:, 128 - lo:256 - lo] - late[:, 128 - lo:256 - lo]
+        x_low = [xb[8:, 128 * h:128 * h + 128] for h in range(2)]
         for g in range(2):
             if g == 0:
                 s = [[spread_row(spl, 8 * j + i, 0) for j in range(i + 1)] for i in range(8)]
@@ -100,17 +106,13 @@
                     mid[8 * j:8 * j + 8, :] = d[j]
                 s = [[spread_row(mid, 8 * j + i, 0) for j in range(i + 1)] for i in range(8)]
                 v = c
+                for h in range(2):
+                    xb[8:, 128 * h:128 * h + 128] = x_low[h]
             x = [[spread_row(xb, 8 * g + i, h) for h in range(2)] for i in range(8)]
-            if g == 1:
-                for k in range(8):
-                    for i in range(8):
-                        for h in range(2):
-                            x[i][h] = x[i][h] - cross[k][i] * y_all[k][h]
             cross = []
             for k in range(8):
                 r = lax.rsqrt(s[k][k])
                 y = [x[k][h] * r for h in range(2)]
-                y_all.append(y)
                 for h in range(2):
                     zb[8 * g + k:8 * g + k + 1, 128 * h:128 * h + 128] = y[h][:1]
                 col = [None] * 8
@@ -128,6 +130,7 @@
                     low[8 * k:8 * k + 8, :] = v[k][0]
                     cross.append([spread_row(low, 8 * k + i, 0) for i in range(8)])
                     below = v[k][1:]
+                    x_low = [t - v[k][0] * u for t, u in zip(x_low, y)]
                     for j in range(8):
                         d[j] = d[j] - v[k][0] * cross[k][j]
                         c[j] = [t - u * cross[k][j] for t, u in zip(c[j], below)]
@@ -141,7 +144,10 @@
         return carry
 
     for top in range(2):
-        lax.fori_loop(top * STEPS // 2, (top + 1) * STEPS // 2, functools.partial(step, top=top), 0)
+        lax.fori_loop(top * STEPS // 4, (top + 1) * STEPS // 4, lambda t, c: step(2 * t + 1, step(2 * t, c, top), top), 0)
+        if top == 0:
+            kept = lax.broadcasted_iota(jnp.int32, (128, 128), 1) < 128 - NB
+            w[128:, :128] = jnp.where(kept, w[128:, :128], 0.0)
 
 
 def kernel(flags, mine, other, panel, trail, trail_other, pf, up, nx, w, inv, *work):
@@ -165,9 +171,8 @@
     corner, block1 = [t.reshape(N, N) for t in pair(8, 24)]
     block2 = jnp.concatenate(pair(24, 32), 1).reshape(N, N)
     inv1 = inv[...]
-    below1 = dot_nt(block1, inv1)
-    corner = corner - dot_nt(below1, below1)
-    corner = 0.5 * (corner + corner.T)
+    below1 = dot_nt6(block1, inv1)
+    corner = 0.5 * (corner + corner.T) - dot_nt6(below1, below1)
     w[...] = corner
     inv1 = split(inv1)
     below_own = split(jnp.where(is0, below1, dot_nt3(block2, inv1)))

time: 68.3 us -> 66.3 us (0.971)
  Pallas kernels: 18.2 us -> 16.2 us
    pallas_call x1, Pallas kernels: 18.2 us -> 16.2 us  [local_part(): pl.pallas_call(kernel, out_shape=[jax.ShapeDtypeStruct((512, N), f32), ja...]
where the time goes in v4:
time: 66.3 us; the launch traced here: 65.9 us
  starting transfers between devices  28 us (42%)
  waiting for transfers between devices  17.3 us (26%)
  Pallas kernels  16.2 us (24%)
  local copies, waits for them, and re-layouts  2.77 us (4%)
  other arithmetic  0.84 us (1%)
  between operations  0.76 us (1%)
    pallas_call x1, Pallas kernels, local_part(): pl.pallas_call(kernel, out_shape=[jax.ShapeDtypeStruct((512, N), f32), ja...  16.2 us
    ppermute x3, starting transfers between devices, on_device(): piece = piece + lax.ppermute(piece, 'z', pairs)  8.44 us
    all_to_all x1, starting transfers between devices, on_device(): got = lax.all_to_all(sent, plane, 0, 0)  7.57 us
    all_to_all x1, waiting for transfers between devices, on_device(): got = lax.all_to_all(sent, plane, 0, 0)  7.54 us
    all_to_all x1, waiting for transfers between devices, on_device(): lax.all_to_all(jnp.broadcast_to(piece[None], (16, 32, N)), plane, 0, 0)  5.31 us
    ppermute x1, starting transfers between devices, on_device(): other = lax.ppermute(mine, 'core', [(0, 1), (1, 0)])  4.64 us
    all_to_all x1, starting transfers between devices, on_device(): lax.all_to_all(jnp.broadcast_to(piece[None], (16, 32, N)), plane, 0, 0)  3.71 us
    ppermute x1, starting transfers between devices, on_device(): trail_other = lax.ppermute(trail.reshape(512, N), 'core', [(0, 1), (1, 0)])  3.62 us
  transfers between devices with their start and end apart: 7, of which 6 were waited for; matrix products, arithmetic and copies ran while one was open for 0% of the time, Pallas kernels for 0%

profile of v4, /device:TPU:1, one launch (start us, length us, event | category | flops | bytes accessed | tf_op | source)
XLA Modules:
  0.0 65.9 jit_solution(9382775602275586311)
XLA Ops:
  0.6 0.0 slice-start.1
  0.6 0.9 %slice-done.1 = f32[1,256,1,256]{3,2,1,0:T(1,128)S(1)} async-done(((f32[2,256,1,256]{3,2,1,0:T(1,128)}), f32[1,256,1,256]{3,2,1,0:T(1,128)S(1)}, s32[]{:S(2)}) %slice-start.1) | async-done | bytes 262168 | tf_op jit(solution)/shard_map/slice | solution.py:260
  1.6 0.0 slice-start
  1.6 0.9 %slice-done = f32[1,256,256]{2,1,0:T(8,128)S(1)} async-done(((f32[2,256,256]{2,1,0:T(8,128)}), f32[1,256,256]{2,1,0:T(8,128)S(1)}, s32[]{:S(2)}) %slice-start) | async-done | bytes 262168 | tf_op jit(solution)/shard_map/slice | solution.py:260
  2.5 0.7 %broadcast_select_fusion = f32[16,16,256]{2,1,0:T(8,128)} fusion(f32[16,16,256]{2,1,0:T(8,128)S(1)} %bitcast.19, f32[16,16,256]{2,1,0:T(8,128)S(1)} %bitcast.18, pred[]{:T(512)S(6)} %and.7), kind=kLoop, calls=%fused_computation | loop fusion | flops 65536 | bytes 786433 | tf_op jit(solution)/shard_map/jit(_where)/select_n | solution.py:260
  3.3 7.6 %all-to-all-start = ((f32[16,16,256]{2,1,0:T(8,128)}), f32[16,16,256]{2,1,0:T(8,128)S(1)}, u32[]{:S(2)}, u32[]{:S(2)}) async-start(f32[16,16,256]{2,1,0:T(8,128)} %broadcast_select_fusion), calls=%async_computation | async-start | bytes 524288 | tf_op jit(solution)/shard_map/all_to_all | solution.py:261
  10.9 7.5 %all-to-all-done = f32[16,16,256]{2,1,0:T(8,128)S(1)} async-done(((f32[16,16,256]{2,1,0:T(8,128)}), f32[16,16,256]{2,1,0:T(8,128)S(1)}, u32[]{:S(2)}, u32[]{:S(2)}) %all-to-all-start) | async-done | bytes 262176 | tf_op jit(solution)/shard_map/all_to_all | solution.py:261
  18.4 3.5 %collective-permute-start = (f32[32,256]{1,0:T(8,128)S(1)}, f32[32,256]{1,0:T(8,128)S(1)}, u32[]{:S(2)}, u32[]{:S(2)}) collective-permute-start(f32[32,256]{1,0:T(8,128)S(1)} %maximum_select_fusion), channel_id=1, source_target_pairs={{0,32},{1,33},{2,34},{3,35},{4,36},{5,37},{6,38},{7,39},{8,40},{9,... | collective-permute-start | bytes 98312 | tf_op jit(solution)/shard_map/ppermute | solution.py:266
  22.0 1.0 %collective-permute-done = f32[32,256]{1,0:T(8,128)S(1)} collective-permute-done((f32[32,256]{1,0:T(8,128)S(1)}, f32[32,256]{1,0:T(8,128)S(1)}, u32[]{:S(2)}, u32[]{:S(2)}) %collective-permute-start) | collective-permute-done | bytes 32800 | tf_op jit(solution)/shard_map/ppermute | solution.py:266
  23.0 3.6 %collective-permute-start.1 = (f32[32,256]{1,0:T(8,128)S(1)}, f32[32,256]{1,0:T(8,128)S(1)}, u32[]{:S(2)}, u32[]{:S(2)}) collective-permute-start(f32[32,256]{1,0:T(8,128)S(1)} %add.17), channel_id=1, source_target_pairs={{0,224},{32,64},{1,225},{33,65},{2,226},{34,66},{3,227},{35,67},{4... | collective-permute-start | bytes 98312 | tf_op jit(solution)/shard_map/ppermute | solution.py:266
  26.6 1.0 %collective-permute-done.1 = f32[32,256]{1,0:T(8,128)S(1)} collective-permute-done((f32[32,256]{1,0:T(8,128)S(1)}, f32[32,256]{1,0:T(8,128)S(1)}, u32[]{:S(2)}, u32[]{:S(2)}) %collective-permute-start.1) | collective-permute-done | bytes 32800 | tf_op jit(solution)/shard_map/ppermute | solution.py:266
  27.6 1.3 %collective-permute-start.2 = (f32[32,256]{1,0:T(8,128)S(1)}, f32[32,256]{1,0:T(8,128)S(1)}, u32[]{:S(2)}, u32[]{:S(2)}) collective-permute-start(f32[32,256]{1,0:T(8,128)S(1)} %add.18), channel_id=1, source_target_pairs={{0,160},{32,128},{64,96},{224,192},{1,161},{33,129},{65,97},{225,1... | collective-permute-start | bytes 98312 | tf_op jit(solution)/shard_map/ppermute | solution.py:266
  28.9 1.0 %collective-permute-done.2 = f32[32,256]{1,0:T(8,128)S(1)} collective-permute-done((f32[32,256]{1,0:T(8,128)S(1)}, f32[32,256]{1,0:T(8,128)S(1)}, u32[]{:S(2)}, u32[]{:S(2)}) %collective-permute-start.2) | collective-permute-done | bytes 32800 | tf_op jit(solution)/shard_map/ppermute | solution.py:266
  29.9 0.8 %broadcast_in_dim.11 = f32[16,32,256]{2,1,0:T(8,128)} broadcast(f32[32,256]{1,0:T(8,128)S(1)} %add.19), dimensions={1,2} | broadcast | bytes 557056 | tf_op jit(solution)/shard_map/broadcast_in_dim | solution.py:267
  30.8 0.0 copy-start.1
  30.8 3.7 %all-to-all-start.1 = ((f32[16,32,256]{2,1,0:T(8,128)}), f32[16,32,256]{2,1,0:T(8,128)S(1)}, u32[]{:S(2)}, u32[]{:S(2)}) async-start(f32[16,32,256]{2,1,0:T(8,128)} %broadcast_in_dim.11), calls=%async_computation.1 | async-start | bytes 1048576 | tf_op jit(solution)/shard_map/all_to_all | solution.py:267
  34.5 0.0 copy-done.1
  34.5 0.0 copy-start
  34.6 3.6 %collective-permute-start.4 = (f32[512,256]{1,0:T(8,128)S(1)}, f32[512,256]{1,0:T(8,128)S(1)}, u32[]{:S(2)}, u32[]{:S(2)}) collective-permute-start(f32[512,256]{1,0:T(8,128)S(1)} %bitcast.15), channel_id=1, source_target_pairs={{0,1},{1,0},{2,3},{3,2},{4,5},{5,4},{6,7},{7,6},{8,9},{9,8},{10,11... | collective-permute-start | bytes 1572872 | tf_op jit(solution)/shard_map/ppermute | solution.py:259
  38.2 5.3 %all-to-all-done.1.mine = f32[16,32,256]{2,1,0:T(8,128)S(1)} async-done(((f32[16,32,256]{2,1,0:T(8,128)}), f32[16,32,256]{2,1,0:T(8,128)S(1)}, u32[]{:S(2)}, u32[]{:S(2)}) %all-to-all-start.1) | async-done | bytes 524320 | tf_op jit(solution)/shard_map/all_to_all | solution.py:267
  43.5 4.6 %collective-permute-start.3 = (f32[16,32,256]{2,1,0:T(8,128)S(1)}, f32[16,32,256]{2,1,0:T(8,128)S(1)}, u32[]{:S(2)}, u32[]{:S(2)}) collective-permute-start(f32[16,32,256]{2,1,0:T(8,128)S(1)} %all-to-all-done.1.mine), channel_id=1, source_target_pairs={{0,1},{1,0},{2,3},{3,2},{4,5},{5,4},{6,7},{7,6},{8,9},{9,8},{10,11... | collective-permute-start | bytes 1572872 | tf_op jit(solution)/shard_map/ppermute | solution.py:268
  48.1 0.1 pad_add_fusion.flags
  48.2 0.0 collective-permute-done.4.trail_other
  48.2 1.5 %collective-permute-done.3.other = f32[16,32,256]{2,1,0:T(8,128)S(1)} collective-permute-done((f32[16,32,256]{2,1,0:T(8,128)S(1)}, f32[16,32,256]{2,1,0:T(8,128)S(1)}, u32[]{:S(2)}, u32[]{:S(2)}) %collective-permute-start.3) | collective-permute-done | bytes 524320 | tf_op jit(solution)/shard_map/ppermute | solution.py:268
  49.7 0.0 copy-done
  49.7 16.2 %panel_step.1 = (f32[512,256]{1,0:T(8,128)}, f32[1024,128]{1,0:T(8,128)}, f32[512,128]{1,0:T(8,128)}) custom-call(s32[2]{0:T(128)S(1)} %pad_add_fusion.flags, f32[16,32,256]{2,1,0:T(8,128)S(1)} %all-to-all-done.1.mine, f32[16,32,256]{2,1,0:T(8,128)S(1)} %collective-permute-done.3.other, f32[512,256]{1,0:T(8,128)S(1)} %bitcast.17, f32[512,256]{1,0:T(8,128)S(1)} %bitcast.16, ...), custom_call_target="tpu_custom_call" | custom-call | tf_op jit(solution)/shard_map/panel_step/pallas_call | solution.py:223
  (9 shorter events, 0.1 us)
Async XLA Ops:
  0.6 1.0 %slice-start.1 = ((f32[2,256,1,256]{3,2,1,0:T(1,128)}), f32[1,256,1,256]{3,2,1,0:T(1,128)S(1)}, s32[]{:S(2)}) async-start(f32[2,256,1,256]{3,2,1,0:T(1,128)} %param.3), calls=%async_computation.3 | async-start | bytes 524288 | tf_op jit(solution)/shard_map/slice | solution.py:260
  1.6 0.9 %slice-start = ((f32[2,256,256]{2,1,0:T(8,128)}), f32[1,256,256]{2,1,0:T(8,128)S(1)}, s32[]{:S(2)}) async-start(f32[2,256,256]{2,1,0:T(8,128)} %param.2), calls=%async_computation.2 | async-start | bytes 524288 | tf_op jit(solution)/shard_map/slice | solution.py:260
  3.3 15.1 %all-to-all-start = ((f32[16,16,256]{2,1,0:T(8,128)}), f32[16,16,256]{2,1,0:T(8,128)S(1)}, u32[]{:S(2)}, u32[]{:S(2)}) async-start(f32[16,16,256]{2,1,0:T(8,128)} %broadcast_select_fusion), calls=%async_computation | async-start | bytes 524288 | tf_op jit(solution)/shard_map/all_to_all | solution.py:261
  18.4 4.6 %collective-permute-start = (f32[32,256]{1,0:T(8,128)S(1)}, f32[32,256]{1,0:T(8,128)S(1)}, u32[]{:S(2)}, u32[]{:S(2)}) collective-permute-start(f32[32,256]{1,0:T(8,128)S(1)} %maximum_select_fusion), channel_id=1, source_target_pairs={{0,32},{1,33},{2,34},{3,35},{4,36},{5,37},{6,38},{7,39},{8,40},{9,... | collective-permute-start | bytes 98312 | tf_op jit(solution)/shard_map/ppermute | solution.py:266
  23.0 4.6 %collective-permute-start.1 = (f32[32,256]{1,0:T(8,128)S(1)}, f32[32,256]{1,0:T(8,128)S(1)}, u32[]{:S(2)}, u32[]{:S(2)}) collective-permute-start(f32[32,256]{1,0:T(8,128)S(1)} %add.17), channel_id=1, source_target_pairs={{0,224},{32,64},{1,225},{33,65},{2,226},{34,66},{3,227},{35,67},{4... | collective-permute-start | bytes 98312 | tf_op jit(solution)/shard_map/ppermute | solution.py:266
  27.6 2.3 %collective-permute-start.2 = (f32[32,256]{1,0:T(8,128)S(1)}, f32[32,256]{1,0:T(8,128)S(1)}, u32[]{:S(2)}, u32[]{:S(2)}) collective-permute-start(f32[32,256]{1,0:T(8,128)S(1)} %add.18), channel_id=1, source_target_pairs={{0,160},{32,128},{64,96},{224,192},{1,161},{33,129},{65,97},{225,1... | collective-permute-start | bytes 98312 | tf_op jit(solution)/shard_map/ppermute | solution.py:266
  30.8 3.7 %copy-start.1 = (f32[2,256,1,256]{3,2,1,0:T(1,128)S(1)}, f32[2,256,1,256]{3,2,1,0:T(1,128)}, u32[]{:S(2)}) copy-start(f32[2,256,1,256]{3,2,1,0:T(1,128)} %param.3) | copy-start | bytes 1572868
  30.8 12.7 %all-to-all-start.1 = ((f32[16,32,256]{2,1,0:T(8,128)}), f32[16,32,256]{2,1,0:T(8,128)S(1)}, u32[]{:S(2)}, u32[]{:S(2)}) async-start(f32[16,32,256]{2,1,0:T(8,128)} %broadcast_in_dim.11), calls=%async_computation.1 | async-start | bytes 1048576 | tf_op jit(solution)/shard_map/all_to_all | solution.py:267
  34.5 15.2 %copy-start = (f32[2,256,256]{2,1,0:T(8,128)S(1)}, f32[2,256,256]{2,1,0:T(8,128)}, u32[]{:S(2)}) copy-start(f32[2,256,256]{2,1,0:T(8,128)} %param.2) | copy-start | bytes 1572868
  34.6 13.6 %collective-permute-start.4 = (f32[512,256]{1,0:T(8,128)S(1)}, f32[512,256]{1,0:T(8,128)S(1)}, u32[]{:S(2)}, u32[]{:S(2)}) collective-permute-start(f32[512,256]{1,0:T(8,128)S(1)} %bitcast.15), channel_id=1, source_target_pairs={{0,1},{1,0},{2,3},{3,2},{4,5},{5,4},{6,7},{7,6},{8,9},{9,8},{10,11... | collective-permute-start | bytes 1572872 | tf_op jit(solution)/shard_map/ppermute | solution.py:259
  43.5 6.2 %collective-permute-start.3 = (f32[16,32,256]{2,1,0:T(8,128)S(1)}, f32[16,32,256]{2,1,0:T(8,128)S(1)}, u32[]{:S(2)}, u32[]{:S(2)}) collective-permute-start(f32[16,32,256]{2,1,0:T(8,128)S(1)} %all-to-all-done.1.mine), channel_id=1, source_target_pairs={{0,1},{1,0},{2,3},{3,2},{4,5},{5,4},{6,7},{7,6},{8,9},{9,8},{10,11... | collective-permute-start | bytes 1572872 | tf_op jit(solution)/shard_map/ppermute | solution.py:268

commit v5 on v4

--- a/solution.py
+++ b/solution.py
@@ -150,27 +150,26 @@
             w[128:, :128] = jnp.where(kept, w[128:, :128], 0.0)
 
 
-def kernel(flags, mine, other, panel, trail, trail_other, pf, up, nx, w, inv, *work):
-    *work, panel_in, solved_out, up_out, nx_out, sems = work
-    fetch = pltpu.make_async_copy(panel, panel_in, sems.at[0])
-    fetch.start()
+def lead_kernel(blocks, inv, w, *work):
+    head = blocks[:, :16, :].reshape(N, N)
+    w[...] = 0.5 * (head + head.T)
+    factor_inverse(w, inv, *work)
+
+
+def kernel(flags, blocks, swapped, inv_lead, panel, trail, trail_other, pf, up, nx, w, inv, *work):
     row, core = flags[0], flags[1]
     is0 = core == 0
     lane_all = lax.broadcasted_iota(jnp.int32, (N, N), 1)
     row_all = lax.broadcasted_iota(jnp.int32, (N, N), 0)
     low = lane_all <= row_all
-
-    def pair(lo, hi):
-        m, o = mine[:, lo:hi, :], other[:, lo:hi, :]
-        return jnp.where(is0, m, o), jnp.where(is0, o, m)
-
-    head = jnp.concatenate(pair(0, 8), 1).reshape(N, N)
-    head = 0.5 * (head + head.T)
-    w[...] = head
-    factor_inverse(w, inv, *work)
-    corner, block1 = [t.reshape(N, N) for t in pair(8, 24)]
-    block2 = jnp.concatenate(pair(24, 32), 1).reshape(N, N)
-    inv1 = inv[...]
+    *work, panel_in, solved_out, up_out, nx_out, sems = work
+    fetch = pltpu.make_async_copy(panel, panel_in, sems.at[0])
+    fetch.start()
+    held, missing = blocks[:, 16:32, :].reshape(N, N), swapped[:, :16, :].reshape(N, N)
+    corner, block1 = jnp.where(is0, held, missing), jnp.where(is0, missing, held)
+    part, rest = blocks[:, 32:, :], swapped[:, 16:, :]
+    block2 = jnp.concatenate([jnp.where(is0, part, rest), jnp.where(is0, rest, part)], 1).reshape(N, N)
+    inv1 = inv_lead[...]
     below1 = dot_nt6(block1, inv1)
     corner = 0.5 * (corner + corner.T) - dot_nt6(below1, below1)
     w[...] = corner
@@ -216,7 +215,33 @@
         copy.wait()
 
 
-def local_part(flags, mine, other, panel, trail, trail_other):
+WORK = [
+    pltpu.VMEM((N, N), jnp.float32),
+    pltpu.VMEM((NB, N), jnp.float32),
+    pltpu.VMEM((64, 128), jnp.float32),
+    pltpu.VMEM((64, 128), jnp.float32),
+    pltpu.VMEM((64, 128), jnp.float32),
+    pltpu.VMEM((NB, N), jnp.float32),
+    pltpu.VMEM((NB, N), jnp.float32),
+    pltpu.VMEM((N, 6 * NB), jnp.bfloat16),
+]
+
+
+def factor_lead(blocks):
+    vmem = pl.BlockSpec(memory_space=pltpu.VMEM)
+    return pl.pallas_call(
+        lead_kernel,
+        out_shape=jax.ShapeDtypeStruct((N, N), jnp.float32),
+        in_specs=[vmem],
+        out_specs=vmem,
+        scratch_shapes=WORK,
+        compiler_params=pltpu.CompilerParams(vmem_limit_bytes=16 << 20),
+        cost_estimate=pl.CostEstimate(flops=4 << 30, bytes_accessed=8 << 20, transcendentals=0),
+        name="factor_lead",
+    )(blocks)
+
+
+def local_part(flags, blocks, swapped, inv_lead, panel, trail, trail_other):
     vmem = pl.BlockSpec(memory_space=pltpu.VMEM)
     anywhere = pl.BlockSpec(memory_space=pl.ANY)
     f32 = jnp.float32
@@ -227,18 +252,9 @@
             jax.ShapeDtypeStruct((1024, 128), f32),
             jax.ShapeDtypeStruct((512, 128), f32),
         ],
-        in_specs=[pl.BlockSpec(memory_space=pltpu.SMEM), vmem, vmem, anywhere, vmem, vmem],
+        in_specs=[pl.BlockSpec(memory_space=pltpu.SMEM), vmem, vmem, vmem, anywhere, vmem, vmem],
         out_specs=[anywhere] * 3,
-        scratch_shapes=[
-            pltpu.VMEM((N, N), f32),
-            pltpu.VMEM((N, N), f32),
-            pltpu.VMEM((NB, N), f32),
-            pltpu.VMEM((64, 128), f32),
-            pltpu.VMEM((64, 128), f32),
-            pltpu.VMEM((64, 128), f32),
-            pltpu.VMEM((NB, N), f32),
-            pltpu.VMEM((NB, N), f32),
-            pltpu.VMEM((N, 6 * NB), jnp.bfloat16),
+        scratch_shapes=WORK[:1] + WORK + [
             pltpu.VMEM((512, N), f32),
             pltpu.VMEM((512, N), f32),
             pltpu.VMEM((1024, 128), f32),
@@ -247,7 +263,7 @@
         ],
         compiler_params=pltpu.CompilerParams(vmem_limit_bytes=40 << 20),
         name="panel_step",
-    )(flags, mine, other, panel, trail, trail_other)
+    )(flags, blocks, swapped, inv_lead, panel, trail, trail_other)
 
 
 def on_device(panel, trail):
@@ -259,16 +275,18 @@
     trail_other = lax.ppermute(trail.reshape(512, N), "core", [(0, 1), (1, 0)])
     sent = jnp.where((row == 1) & (core == 0), trail[0, :, 0, :], panel[0]).reshape(16, 16, N)
     got = lax.all_to_all(sent, plane, 0, 0)
-    shares = jnp.where(core == 0, got[:3:2, :8], got[:3:2, 8:])
-    piece = jnp.concatenate([shares[0], got[1], shares[1]], 0)
+    share = jnp.where(core == 0, got[2, :8], got[2, 8:])
+    piece = jnp.concatenate([got[0], got[1], share], 0)
     piece = jnp.where(z == 0, piece, 0.0)
     for pairs in Z_STEPS:
         piece = piece + lax.ppermute(piece, "z", pairs)
-    mine = lax.all_to_all(jnp.broadcast_to(piece[None], (16, 32, N)), plane, 0, 0)
-    other = lax.ppermute(mine, "core", [(0, 1), (1, 0)])
+    blocks = lax.all_to_all(jnp.broadcast_to(piece[None], (16, 40, N)), plane, 0, 0)
+    swapped = lax.ppermute(blocks[:, 16:], "core", [(0, 1), (1, 0)])
+    inv_lead = factor_lead(blocks)
     flags = jnp.stack([row, core]).astype(jnp.int32)
     pf, up, nx = local_part(
-        flags, mine, other, panel.reshape(512, N), trail.reshape(512, N), trail_other
+        flags, blocks, swapped, inv_lead,
+        panel.reshape(512, N), trail.reshape(512, N), trail_other,
     )
     return pf.reshape(2, N, N), up.reshape(2, N, 1, N), nx.reshape(2, N, 128)
 

time: 66.3 us -> 65.9 us (level)
    pallas_call x1, Pallas kernels: 16.2 us -> 10 us  [local_part(): pl.pallas_call(kernel, out_shape=[jax.ShapeDtypeStruct((512, N), f32), ja...]
    pallas_call x0 -> x1, Pallas kernels: none -> 6.16 us  [factor_lead(): pl.pallas_call(lead_kernel, out_shape=jax.ShapeDtypeStruct((N, N), jnp.fl...]
    ppermute x1, waiting for transfers between devices: 1.46 us -> 0.01 us  [on_device(): swapped = lax.ppermute(blocks[:, 16:], 'core', [(0, 1), (1, 0)])]
  transfers between devices with their start and end apart: 7 -> 7, of which waited for: 6 -> 5; matrix products, arithmetic and copies ran while one was open for 0% -> 0% of each run, Pallas kernels for 0% -> 9%
where the time goes in v5:
time: 65.9 us; the launch traced here: 65.5 us
  starting transfers between devices  28.1 us (43%)
  waiting for transfers between devices  16.8 us (25%)
  Pallas kernels  16.2 us (25%)
  local copies, waits for them, and re-layouts  2.83 us (4%)
  other arithmetic  0.84 us (1%)
  between operations  0.79 us (1%)
    pallas_call x1, Pallas kernels, local_part(): pl.pallas_call(kernel, out_shape=[jax.ShapeDtypeStruct((512, N), f32), ja...  10 us
    ppermute x3, starting transfers between devices, on_device(): piece = piece + lax.ppermute(piece, 'z', pairs)  8.36 us
    all_to_all x1, starting transfers between devices, on_device(): got = lax.all_to_all(sent, plane, 0, 0)  7.57 us
    all_to_all x1, waiting for transfers between devices, on_device(): got = lax.all_to_all(sent, plane, 0, 0)  7.54 us
    pallas_call x1, Pallas kernels, factor_lead(): pl.pallas_call(lead_kernel, out_shape=jax.ShapeDtypeStruct((N, N), jnp.fl...  6.16 us
    all_to_all x1, waiting for transfers between devices, on_device(): lax.all_to_all(jnp.broadcast_to(piece[None], (16, 40, N)), plane, 0, 0)  5.9 us
    ppermute x1, starting transfers between devices, on_device(): swapped = lax.ppermute(blocks[:, 16:], 'core', [(0, 1), (1, 0)])  4.77 us
    all_to_all x1, starting transfers between devices, on_device(): lax.all_to_all(jnp.broadcast_to(piece[None], (16, 40, N)), plane, 0, 0)  3.72 us
  transfers between devices with their start and end apart: 7, of which 5 were waited for; matrix products, arithmetic and copies ran while one was open for 0% of the time, Pallas kernels for 9%

profile of v5, /device:TPU:1, one launch (start us, length us, event | category | flops | bytes accessed | tf_op | source)
XLA Modules:
  0.0 65.5 jit_solution(3446566942555933720)
XLA Ops:
  0.6 0.0 slice-start.1
  0.6 0.9 %slice-done.1 = f32[1,256,1,256]{3,2,1,0:T(1,128)S(1)} async-done(((f32[2,256,1,256]{3,2,1,0:T(1,128)}), f32[1,256,1,256]{3,2,1,0:T(1,128)S(1)}, s32[]{:S(2)}) %slice-start.1) | async-done | bytes 262168 | tf_op jit(solution)/shard_map/slice | solution.py:276
  1.6 0.0 slice-start
  1.6 0.9 %slice-done = f32[1,256,256]{2,1,0:T(8,128)S(1)} async-done(((f32[2,256,256]{2,1,0:T(8,128)}), f32[1,256,256]{2,1,0:T(8,128)S(1)}, s32[]{:S(2)}) %slice-start) | async-done | bytes 262168 | tf_op jit(solution)/shard_map/slice | solution.py:276
  2.5 0.7 %broadcast_select_fusion = f32[16,16,256]{2,1,0:T(8,128)} fusion(f32[16,16,256]{2,1,0:T(8,128)S(1)} %bitcast.19, f32[16,16,256]{2,1,0:T(8,128)S(1)} %bitcast.18, pred[]{:T(512)S(6)} %and.7), kind=kLoop, calls=%fused_computation | loop fusion | flops 65536 | bytes 786433 | tf_op jit(solution)/shard_map/jit(_where)/select_n | solution.py:276
  3.3 7.6 %all-to-all-start = ((f32[16,16,256]{2,1,0:T(8,128)}), f32[16,16,256]{2,1,0:T(8,128)S(1)}, u32[]{:S(2)}, u32[]{:S(2)}) async-start(f32[16,16,256]{2,1,0:T(8,128)} %broadcast_select_fusion), calls=%async_computation | async-start | bytes 524288 | tf_op jit(solution)/shard_map/all_to_all | solution.py:277
  10.9 7.5 %all-to-all-done = f32[16,16,256]{2,1,0:T(8,128)S(1)} async-done(((f32[16,16,256]{2,1,0:T(8,128)}), f32[16,16,256]{2,1,0:T(8,128)S(1)}, u32[]{:S(2)}, u32[]{:S(2)}) %all-to-all-start) | async-done | bytes 262176 | tf_op jit(solution)/shard_map/all_to_all | solution.py:277
  18.4 3.5 %collective-permute-start = (f32[40,256]{1,0:T(8,128)S(1)}, f32[40,256]{1,0:T(8,128)S(1)}, u32[]{:S(2)}, u32[]{:S(2)}) collective-permute-start(f32[40,256]{1,0:T(8,128)S(1)} %maximum_select_fusion), channel_id=1, source_target_pairs={{0,32},{1,33},{2,34},{3,35},{4,36},{5,37},{6,38},{7,39},{8,40},{9,... | collective-permute-start | bytes 122888 | tf_op jit(solution)/shard_map/ppermute | solution.py:282
  22.0 1.1 %collective-permute-done = f32[40,256]{1,0:T(8,128)S(1)} collective-permute-done((f32[40,256]{1,0:T(8,128)S(1)}, f32[40,256]{1,0:T(8,128)S(1)}, u32[]{:S(2)}, u32[]{:S(2)}) %collective-permute-start) | collective-permute-done | bytes 40992 | tf_op jit(solution)/shard_map/ppermute | solution.py:282
  23.1 3.5 %collective-permute-start.1 = (f32[40,256]{1,0:T(8,128)S(1)}, f32[40,256]{1,0:T(8,128)S(1)}, u32[]{:S(2)}, u32[]{:S(2)}) collective-permute-start(f32[40,256]{1,0:T(8,128)S(1)} %add.17), channel_id=1, source_target_pairs={{0,224},{32,64},{1,225},{33,65},{2,226},{34,66},{3,227},{35,67},{4... | collective-permute-start | bytes 122888 | tf_op jit(solution)/shard_map/ppermute | solution.py:282
  26.6 1.1 %collective-permute-done.1 = f32[40,256]{1,0:T(8,128)S(1)} collective-permute-done((f32[40,256]{1,0:T(8,128)S(1)}, f32[40,256]{1,0:T(8,128)S(1)}, u32[]{:S(2)}, u32[]{:S(2)}) %collective-permute-start.1) | collective-permute-done | bytes 40992 | tf_op jit(solution)/shard_map/ppermute | solution.py:282
  27.7 1.3 %collective-permute-start.2 = (f32[40,256]{1,0:T(8,128)S(1)}, f32[40,256]{1,0:T(8,128)S(1)}, u32[]{:S(2)}, u32[]{:S(2)}) collective-permute-start(f32[40,256]{1,0:T(8,128)S(1)} %add.18), channel_id=1, source_target_pairs={{0,160},{32,128},{64,96},{224,192},{1,161},{33,129},{65,97},{225,1... | collective-permute-start | bytes 122888 | tf_op jit(solution)/shard_map/ppermute | solution.py:282
  29.0 1.2 %collective-permute-done.2 = f32[40,256]{1,0:T(8,128)S(1)} collective-permute-done((f32[40,256]{1,0:T(8,128)S(1)}, f32[40,256]{1,0:T(8,128)S(1)}, u32[]{:S(2)}, u32[]{:S(2)}) %collective-permute-start.2) | collective-permute-done | bytes 40992 | tf_op jit(solution)/shard_map/ppermute | solution.py:282
  30.2 0.9 %broadcast_in_dim.11 = f32[16,40,256]{2,1,0:T(8,128)} broadcast(f32[40,256]{1,0:T(8,128)S(1)} %add.19), dimensions={1,2} | broadcast | bytes 696320 | tf_op jit(solution)/shard_map/broadcast_in_dim | solution.py:283
  31.1 0.0 copy-start.1
  31.1 3.7 %all-to-all-start.1 = ((f32[16,40,256]{2,1,0:T(8,128)}), f32[16,40,256]{2,1,0:T(8,128)S(1)}, u32[]{:S(2)}, u32[]{:S(2)}) async-start(f32[16,40,256]{2,1,0:T(8,128)} %broadcast_in_dim.11), calls=%async_computation.1 | async-start | bytes 1310720 | tf_op jit(solution)/shard_map/all_to_all | solution.py:283
  34.8 0.0 copy-done.1
  34.9 3.6 %collective-permute-start.4 = (f32[512,256]{1,0:T(8,128)S(1)}, f32[512,256]{1,0:T(8,128)S(1)}, u32[]{:S(2)}, u32[]{:S(2)}) collective-permute-start(f32[512,256]{1,0:T(8,128)S(1)} %bitcast.15), channel_id=1, source_target_pairs={{0,1},{1,0},{2,3},{3,2},{4,5},{5,4},{6,7},{7,6},{8,9},{9,8},{10,11... | collective-permute-start | bytes 1572872 | tf_op jit(solution)/shard_map/ppermute | solution.py:275
  38.5 0.1 pad_add_fusion.flags
  38.6 5.9 %all-to-all-done.1.blocks = f32[16,40,256]{2,1,0:T(8,128)S(1)} async-done(((f32[16,40,256]{2,1,0:T(8,128)}), f32[16,40,256]{2,1,0:T(8,128)S(1)}, u32[]{:S(2)}, u32[]{:S(2)}) %all-to-all-start.1) | async-done | bytes 655392 | tf_op jit(solution)/shard_map/all_to_all | solution.py:283
  44.5 0.0 copy-start
  44.5 4.8 %collective-permute-start.3 = (f32[16,24,256]{2,1,0:T(8,128)S(1)}, f32[16,24,256]{2,1,0:T(8,128)S(1)}, u32[]{:S(2)}, u32[]{:S(2)}) collective-permute-start(f32[16,24,256]{2,1,0:T(8,128)S(1)} %slice.32), channel_id=1, source_target_pairs={{0,1},{1,0},{2,3},{3,2},{4,5},{5,4},{6,7},{7,6},{8,9},{9,8},{10,11... | collective-permute-start | bytes 1179656 | tf_op jit(solution)/shard_map/ppermute | solution.py:284
  49.3 6.2 %factor_lead.1.inv_lead = f32[256,256]{1,0:T(8,128)S(1)} custom-call(f32[16,40,256]{2,1,0:T(8,128)S(1)} %all-to-all-done.1.blocks), custom_call_target="tpu_custom_call" | custom-call | flops 4294967296 | bytes 8388608 | tf_op jit(solution)/shard_map/factor_lead/pallas_call | solution.py:232
  55.4 0.0 collective-permute-done.4.trail_other
  55.4 0.0 collective-permute-done.3.swapped
  55.5 0.0 copy-done
  55.5 10.0 %panel_step.1 = (f32[512,256]{1,0:T(8,128)}, f32[1024,128]{1,0:T(8,128)}, f32[512,128]{1,0:T(8,128)}) custom-call(s32[2]{0:T(128)S(1)} %pad_add_fusion.flags, f32[16,40,256]{2,1,0:T(8,128)S(1)} %all-to-all-done.1.blocks, f32[16,24,256]{2,1,0:T(8,128)S(1)} %collective-permute-done.3.swapped, f32[256,256]{1,0:T(8,128)S(1)} %factor_lead.1.inv_lead, ...), custom_call_target="tpu_custom_call" | custom-call | tf_op jit(solution)/shard_map/panel_step/pallas_call | solution.py:248
  (9 shorter events, 0.1 us)
Async XLA Ops:
  0.6 1.0 %slice-start.1 = ((f32[2,256,1,256]{3,2,1,0:T(1,128)}), f32[1,256,1,256]{3,2,1,0:T(1,128)S(1)}, s32[]{:S(2)}) async-start(f32[2,256,1,256]{3,2,1,0:T(1,128)} %param.3), calls=%async_computation.3 | async-start | bytes 524288 | tf_op jit(solution)/shard_map/slice | solution.py:276
  1.6 0.9 %slice-start = ((f32[2,256,256]{2,1,0:T(8,128)}), f32[1,256,256]{2,1,0:T(8,128)S(1)}, s32[]{:S(2)}) async-start(f32[2,256,256]{2,1,0:T(8,128)} %param.2), calls=%async_computation.2 | async-start | bytes 524288 | tf_op jit(solution)/shard_map/slice | solution.py:276
  3.3 15.1 %all-to-all-start = ((f32[16,16,256]{2,1,0:T(8,128)}), f32[16,16,256]{2,1,0:T(8,128)S(1)}, u32[]{:S(2)}, u32[]{:S(2)}) async-start(f32[16,16,256]{2,1,0:T(8,128)} %broadcast_select_fusion), calls=%async_computation | async-start | bytes 524288 | tf_op jit(solution)/shard_map/all_to_all | solution.py:277
  18.4 4.6 %collective-permute-start = (f32[40,256]{1,0:T(8,128)S(1)}, f32[40,256]{1,0:T(8,128)S(1)}, u32[]{:S(2)}, u32[]{:S(2)}) collective-permute-start(f32[40,256]{1,0:T(8,128)S(1)} %maximum_select_fusion), channel_id=1, source_target_pairs={{0,32},{1,33},{2,34},{3,35},{4,36},{5,37},{6,38},{7,39},{8,40},{9,... | collective-permute-start | bytes 122888 | tf_op jit(solution)/shard_map/ppermute | solution.py:282
  23.1 4.6 %collective-permute-start.1 = (f32[40,256]{1,0:T(8,128)S(1)}, f32[40,256]{1,0:T(8,128)S(1)}, u32[]{:S(2)}, u32[]{:S(2)}) collective-permute-start(f32[40,256]{1,0:T(8,128)S(1)} %add.17), channel_id=1, source_target_pairs={{0,224},{32,64},{1,225},{33,65},{2,226},{34,66},{3,227},{35,67},{4... | collective-permute-start | bytes 122888 | tf_op jit(solution)/shard_map/ppermute | solution.py:282
  27.7 2.5 %collective-permute-start.2 = (f32[40,256]{1,0:T(8,128)S(1)}, f32[40,256]{1,0:T(8,128)S(1)}, u32[]{:S(2)}, u32[]{:S(2)}) collective-permute-start(f32[40,256]{1,0:T(8,128)S(1)} %add.18), channel_id=1, source_target_pairs={{0,160},{32,128},{64,96},{224,192},{1,161},{33,129},{65,97},{225,1... | collective-permute-start | bytes 122888 | tf_op jit(solution)/shard_map/ppermute | solution.py:282
  31.1 3.7 %copy-start.1 = (f32[2,256,1,256]{3,2,1,0:T(1,128)S(1)}, f32[2,256,1,256]{3,2,1,0:T(1,128)}, u32[]{:S(2)}) copy-start(f32[2,256,1,256]{3,2,1,0:T(1,128)} %param.3) | copy-start | bytes 1572868
  31.1 13.4 %all-to-all-start.1 = ((f32[16,40,256]{2,1,0:T(8,128)}), f32[16,40,256]{2,1,0:T(8,128)S(1)}, u32[]{:S(2)}, u32[]{:S(2)}) async-start(f32[16,40,256]{2,1,0:T(8,128)} %broadcast_in_dim.11), calls=%async_computation.1 | async-start | bytes 1310720 | tf_op jit(solution)/shard_map/all_to_all | solution.py:283
  34.9 20.6 %collective-permute-start.4 = (f32[512,256]{1,0:T(8,128)S(1)}, f32[512,256]{1,0:T(8,128)S(1)}, u32[]{:S(2)}, u32[]{:S(2)}) collective-permute-start(f32[512,256]{1,0:T(8,128)S(1)} %bitcast.15), channel_id=1, source_target_pairs={{0,1},{1,0},{2,3},{3,2},{4,5},{5,4},{6,7},{7,6},{8,9},{9,8},{10,11... | collective-permute-start | bytes 1572872 | tf_op jit(solution)/shard_map/ppermute | solution.py:275
  44.5 11.0 %copy-start = (f32[2,256,256]{2,1,0:T(8,128)S(1)}, f32[2,256,256]{2,1,0:T(8,128)}, u32[]{:S(2)}) copy-start(f32[2,256,256]{2,1,0:T(8,128)} %param.2) | copy-start | bytes 1572868
  44.5 10.9 %collective-permute-start.3 = (f32[16,24,256]{2,1,0:T(8,128)S(1)}, f32[16,24,256]{2,1,0:T(8,128)S(1)}, u32[]{:S(2)}, u32[]{:S(2)}) collective-permute-start(f32[16,24,256]{2,1,0:T(8,128)S(1)} %slice.32), channel_id=1, source_target_pairs={{0,1},{1,0},{2,3},{3,2},{4,5},{5,4},{6,7},{7,6},{8,9},{9,8},{10,11... | collective-permute-start | bytes 1179656 | tf_op jit(solution)/shard_map/ppermute | solution.py:284
